TPU v7x, 256 devices: a whole 4x4x8 slice. The times are simulated.
256 devices in a mesh: seq: 16 (over z_lo, x), dp: 4 (over y), tp: 4 (over z_hi, core).
Axes of the slice: x: 4, y: 4, z: 8 (z_hi: 2, z_lo: 4; z = z_hi * 4 + z_lo), core: 2. Of those that a mesh axis runs over, the one named last changes fastest.
Arguments:
- patches: bfloat16 [16, 3072, 1152], P(('dp', 'tp'), 'seq'), parts along dimension 0, may hold values from -6 to 6
- seg_ids: int32 [16, 3072], P(('dp', 'tp'), 'seq'), parts along dimension 0, may hold values from 0 to 11, never falling along the last dimension, each value on 1 to 768 neighbouring positions
- pos_rows: int32 [16, 3072], P(('dp', 'tp'), 'seq'), parts along dimension 0, may hold values from 0 to 63
- pos_cols: int32 [16, 3072], P(('dp', 'tp'), 'seq'), parts along dimension 0, may hold values from 0 to 63
- row_table: bfloat16 [64, 1152], replicated, may hold values from -3 to 3
- col_table: bfloat16 [64, 1152], replicated, may hold values from -3 to 3
- ln1_gain: float32 [1152], replicated, may hold values from 0.5 to 1.5
- ln1_bias: float32 [1152], replicated, may hold values from -1.75 to 1.75
- w_qkv: bfloat16 [1152, 3456], P(None, 'seq'), may hold values from -0.41247896 to 0.41247896
- w_out: bfloat16 [1152, 1152], P('seq'), may hold values from -0.1875 to 0.1875
- out_bias: bfloat16 [1152], replicated, may hold values from -3 to 3
- ln2_gain: float32 [1152], replicated, may hold values from 0.5 to 1.5
- ln2_bias: float32 [1152], replicated, may hold values from -1.75 to 1.75
- w_fc1: bfloat16 [1152, 4304], P(None, 'tp'), may hold values from -0.1875 to 0.1875
- fc1_bias: bfloat16 [4304], P('tp'), may hold values from -3 to 3
- w_fc2: bfloat16 [4304, 1152], P('tp'), may hold values from -0.09375 to 0.09375
- fc2_bias: bfloat16 [1152], replicated, may hold values from -3 to 3
Outputs:
- encoded: bfloat16 [16, 3072, 1152], P(('dp', 'tp'), 'seq'), parts along dimension 0
There are 4 independent parts, one for each index of `dp`. A program takes and returns all parts, laid end to end along the dimension named above; an argument that names none is the same for every part. Nothing has to cross between parts.
Inputs may be any that keep to these rules, and one draw needn't show every extreme that they name: `seg_ids`: image numbers never fall along a sequence; every image has 1 to 768 tokens.
All inputs are finite; a program needn't handle non-finite values.
Results may differ from a plain program's by a relative error of at most 0.0095.
Values may be sent and summed in bfloat16 or wider, within the bound.
A program may use at most 64 MiB of HBM per device.

v0:
```python
import math

import jax
import jax.numpy as jnp
from jax import lax
from jax.sharding import Mesh
from jax.sharding import PartitionSpec as P

HEADS = 16
SEQ = ("seq_0", "seq_1")


def sent_to_all(value, axis):
    size = lax.axis_size(axis)
    return lax.all_to_all(
        jnp.broadcast_to(value[None], (size, *value.shape)), axis, 0, 0, tiled=True
    )


def joined_along(blocks, dim):
    blocks = jnp.moveaxis(blocks, 0, dim)
    dims = blocks.shape
    return blocks.reshape(*dims[:dim], dims[dim] * dims[dim + 1], *dims[dim + 2 :])


def collect(value, axis, dim):
    blocks = sent_to_all(value, axis)
    return joined_along(blocks, dim)


def all_blocks(value, axes, sequence):
    blocks = value[None]
    for k in sequence:
        blocks = lax.all_gather(blocks, axes[k], axis=0, tiled=True)
    held = [lax.axis_size(axes[k]) for k in reversed(sequence)]
    blocks = blocks.reshape(*held, *value.shape)
    turned = sorted(range(len(sequence)), key=lambda place: sequence[len(sequence) - 1 - place])
    return blocks.transpose(*turned, *range(len(sequence), blocks.ndim)).reshape(-1, *value.shape)


def gather_axes(value, axes, sequence, dim):
    return joined_along(all_blocks(value, axes, sequence), dim)


def layer_norm(values, gain, shift):
    center = jnp.mean(values, -1, keepdims=True)
    spread = jnp.mean(jnp.square(values - center), -1, keepdims=True)
    return (values - center) * lax.rsqrt(spread + 1e-06) * gain + shift


def attend_head(item, segments):
    length = item.shape[0]
    head_dim = item.shape[1] // 3
    block = min(512, length)
    query = item[:, :head_dim].reshape(length // block, block, head_dim)
    seg_query = segments.reshape(length // block, block)
    keys = item[:, head_dim : 2 * head_dim]
    value = item[:, 2 * head_dim :]

    def one_block(pair):
        rows, seg_rows = pair
        scores = lax.dot_general(
            rows, keys, (((1,), (1,)), ((), ())), preferred_element_type=jnp.float32
        ) / math.sqrt(head_dim)
        same = seg_rows[:, None] == segments[None, :]
        scores = jnp.where(same, scores, -jnp.inf)
        top = jnp.max(scores, -1, keepdims=True)
        expo = jnp.exp(scores - top)
        probs = (expo / jnp.sum(expo, -1, keepdims=True)).astype(jnp.bfloat16)
        return jnp.dot(probs, value, preferred_element_type=jnp.float32).astype(jnp.bfloat16)

    return lax.map(one_block, (query, seg_query)).reshape(length, head_dim)


def per_device(
    patches,
    seg_ids,
    pos_rows,
    pos_cols,
    row_table,
    col_table,
    ln1_gain,
    ln1_bias,
    w_qkv,
    w_out,
    out_bias,
    ln2_gain,
    ln2_bias,
    w_fc1,
    fc1_bias,
    w_fc2,
    fc2_bias,
):
    width = patches.shape[2]
    head_dim = width // HEADS
    heads_here = w_qkv.shape[1] // (3 * head_dim)
    levels = jnp.arange(row_table.shape[0], dtype=jnp.int32)
    row_hot = (pos_rows[0][:, None] == levels[None, :]).astype(jnp.bfloat16)
    col_hot = (pos_cols[0][:, None] == levels[None, :]).astype(jnp.bfloat16)
    embedded = patches[0].astype(jnp.float32) + jnp.dot(
        row_hot, row_table, preferred_element_type=jnp.float32
    )
    embedded = embedded + jnp.dot(col_hot, col_table, preferred_element_type=jnp.float32)
    normed = layer_norm(embedded, ln1_gain, ln1_bias).astype(jnp.bfloat16)
    seg_all = collect(seg_ids[0], SEQ, 0)
    qkv = jnp.dot(
        lax.all_gather(normed, SEQ, axis=0, tiled=True), w_qkv, preferred_element_type=jnp.float32
    ).astype(jnp.bfloat16)
    mixed = jax.vmap(attend_head, in_axes=(1, None), out_axes=1)(
        qkv.reshape(qkv.shape[0], heads_here, 3 * head_dim), seg_all
    )
    mixed = mixed.reshape(mixed.shape[0], heads_here * head_dim)
    returned = lax.all_to_all(mixed, SEQ, split_axis=0, concat_axis=1, tiled=True)
    projected = jnp.dot(
        returned, gather_axes(w_out, SEQ, (0, 1), 0), preferred_element_type=jnp.float32
    )
    attended = embedded + projected + out_bias.astype(jnp.float32)
    normed2 = layer_norm(attended, ln2_gain, ln2_bias).astype(jnp.bfloat16)
    inner = jnp.dot(
        collect(normed2, "tp", 0), w_fc1, preferred_element_type=jnp.float32
    ) + fc1_bias.astype(jnp.float32)
    hidden = jax.nn.gelu(inner, approximate=True).astype(jnp.bfloat16)
    reduced = lax.psum_scatter(
        jnp.dot(hidden, w_fc2, preferred_element_type=jnp.float32).astype(jnp.bfloat16),
        "tp",
        scatter_dimension=0,
        tiled=True,
    ).astype(jnp.float32)
    encoded = (attended + reduced + fc2_bias.astype(jnp.float32)).astype(jnp.bfloat16)
    return encoded[None]


def solution(mesh):
    torus = Mesh(
        mesh.devices.reshape(4, 4, mesh.shape["dp"], mesh.shape["tp"]),
        ("seq_0", "seq_1", "dp", "tp"),
    )
    in_specs = (
        P(("dp", "tp"), SEQ, None),
        P(("dp", "tp"), SEQ),
        P(("dp", "tp"), SEQ),
        P(("dp", "tp"), SEQ),
        P(),
        P(),
        P(),
        P(),
        P(None, SEQ),
        P(SEQ, None),
        P(),
        P(),
        P(),
        P(None, "tp"),
        P("tp"),
        P("tp", None),
        P(),
    )
    out_specs = P(("dp", "tp"), SEQ, None)
    return jax.shard_map(
        per_device, mesh=torus, in_specs=in_specs, out_specs=out_specs, check_vma=False
    )
```

profile of v0, /device:TPU:1, one launch (start us, length us, event | category | flops | bytes accessed | tf_op | source)
XLA Modules:
  0.0 314.2 jit_solution(12667053288190271197)
XLA Ops:
  11.5 9.1 %all-to-all-start = ((s32[16,1,192]{2,1,0:T(1,128)}), s32[16,1,192]{2,1,0:T(1,128)}, u32[]{:S(2)}, u32[]{:S(2)}) async-start(s32[16,1,192]{2,1,0:T(1,128)} %broadcast_in_dim.24), calls=%async_computation | async-start | bytes 32768 | tf_op jit(solution)/shard_map/all_to_all | solution.py:15
  20.6 22.0 %all-gather = bf16[288,1152]{1,0:T(8,128)(2,1)} all-gather(bf16[72,1152]{1,0:T(8,128)(2,1)S(1)} %copy-done.4), channel_id=2, replica_groups=mesh['seq_0'=4,'seq_1'=4,'dp'=4,'tp'=4] {'seq_0'}, dimensions={0}, use_global_device_ids=true | all-gather | bytes 829440 | tf_op jit(solution)/shard_map/all_gather | solution.py:34
  44.3 66.3 %all-gather.4.cloned.1.call-done = bf16[3072,1152]{1,0:T(8,128)(2,1)} async-done(((bf16[192,1152]{1,0:T(8,128)(2,1)}), bf16[3072,1152]{1,0:T(8,128)(2,1)}) %all-gather.4.cloned.1.call-update) | async-done | bytes 7077904 | tf_op jit(solution)/shard_map/all_gather | solution.py:107
  110.7 5.5 %fusion.10 = bf16[3072,1,216]{0,2,1:T(8,128)(2,1)S(1)} fusion(bf16[3072,1152]{1,0:T(8,128)(2,1)} %all-gather.4.cloned.1.call-done, bf16[1152,216]{0,1:T(8,128)(2,1)} %param.27), kind=kOutput, calls=%fused_computation.17 | convolution fusion | flops 1529487360 | bytes 8902656 | tf_op jit(solution)/shard_map/dot_general | solution.py:106
  117.3 2.2 copy.38
  119.5 2.2 copy.33
  121.7 2.2 copy.34
  123.8 34.1 %while.11 = (s32[]{:T(128)}, bf16[6,1,512,72]{2,3,1,0:T(8,128)(2,1)}, s32[6,512]{1,0:T(8,128)S(1)}, s32[16,192]{1,0:T(8,128)}, bf16[6,1,512,72]{3,2,1,0:T(8,128)...) while((s32[]{:T(128)}, ...), condition=%wide.wide.region_5.6_spmd, body=%wide.wide.region_2.5_spmd.sunk | while | flops 467176448 | bytes 22107260 | solution.py:72
  123.8 2.4 fusion.48
  127.4 2.1 fusion.50
  129.5 2.5 fusion.48
  133.1 2.1 fusion.50
  135.3 2.4 fusion.48
  138.8 2.1 fusion.50
  140.9 2.4 fusion.48
  144.5 2.1 fusion.50
  146.6 2.4 fusion.48
  150.1 2.1 fusion.50
  152.3 2.4 fusion.48
  155.8 2.1 fusion.50
  157.9 2.0 copy.35
  159.9 2.5 all_to_all.25
  162.4 2.1 copy.36
  164.5 4.8 %all-to-all-start.1 = ((bf16[16,192,72]{1,2,0:T(8,128)(2,1)}), bf16[16,192,72]{1,2,0:T(8,128)(2,1)}, u32[]{:S(2)}, u32[]{:S(2)}) async-start(bf16[16,192,72]{1,2,0:T(8,128)(2,1)} %copy.36), calls=%async_computation.1 | async-start | bytes 1179648 | tf_op jit(solution)/shard_map/all_to_all | solution.py:113
  169.3 3.5 %copy.37 = bf16[4,4,72,1152]{3,2,1,0:T(8,128)(2,1)} copy(bf16[4,4,72,1152]{3,2,0,1:T(8,128)(2,1)} %bitcast.73) | data formatting | bytes 5308416 | tf_op jit(solution)/shard_map/transpose | solution.py:38
  172.8 8.2 %all-to-all-done.1 = bf16[16,192,72]{1,2,0:T(8,128)(2,1)} async-done(((bf16[16,192,72]{1,2,0:T(8,128)(2,1)}), bf16[16,192,72]{1,2,0:T(8,128)(2,1)}, u32[]{:S(2)}, u32[]{:S(2)}) %all-to-all-start.1) | async-done | bytes 442400 | tf_op jit(solution)/shard_map/all_to_all | solution.py:113
  181.0 2.9 fusion.29
  186.4 12.7 %all-to-all-start.2 = ((bf16[4,192,1152]{2,1,0:T(8,128)(2,1)}), bf16[4,192,1152]{2,1,0:T(8,128)(2,1)}, u32[]{:S(2)}, u32[]{:S(2)}) async-start(bf16[4,192,1152]{2,1,0:T(8,128)(2,1)} %broadcast_in_dim.26), calls=%async_computation.2 | async-start | bytes 3538944 | tf_op jit(solution)/shard_map/all_to_all | solution.py:15
  199.2 33.6 %all-to-all-done.2 = bf16[4,192,1152]{2,1,0:T(8,128)(2,1)} async-done(((bf16[4,192,1152]{2,1,0:T(8,128)(2,1)}), bf16[4,192,1152]{2,1,0:T(8,128)(2,1)}, u32[]{:S(2)}, u32[]{:S(2)}) %all-to-all-start.2) | async-done | bytes 1769504 | tf_op jit(solution)/shard_map/all_to_all | solution.py:15
  232.8 13.3 %convolution_convert_fusion.1 = bf16[768,1152]{1,0:T(8,128)(2,1)} fusion(bf16[1076,1152]{1,0:T(8,128)(2,1)S(1)} %copy-done, bf16[768,1152]{1,0:T(8,128)(2,1)} %bitcast.19, bf16[1152,1076]{0,1:T(8,128)(2,1)} %param.32, f32[1076]{0:T(1024)S(1)} %convert_element_type.52), kind=kOutput, calls=%fused_computation.18 | convolution fusion | flops 3817052160 | bytes 8501456 | tf_op jit(solution)/shard_map/dot_general | solution.py:124
  246.1 59.7 %reduce-scatter.2.cloned.1.call-done = bf16[192,1152]{1,0:T(8,128)(2,1)} async-done(((bf16[768,1152]{1,0:T(8,128)(2,1)}), bf16[192,1152]{1,0:T(8,128)(2,1)}) %reduce-scatter.2.cloned.1.call-update) | async-done | bytes 442384 | tf_op jit(solution)/shard_map/reduce_scatter | solution.py:123
  305.8 1.9 fusion.20
  (79 shorter events, 17.1 us)
Async XLA Ops:
  6.5 226.3 %copy-start = (bf16[1076,1152]{1,0:T(8,128)(2,1)S(1)}, bf16[1076,1152]{1,0:T(8,128)(2,1)}, u32[]{:S(2)}) copy-start(bf16[1076,1152]{1,0:T(8,128)(2,1)} %param.34) | copy-start | bytes 7437316
  6.5 3.3 %copy-start.6 = (f32[1152]{0:T(1024)S(1)}, f32[1152]{0:T(1024)}, u32[]{:S(2)}) copy-start(f32[1152]{0:T(1024)} %param.26) | copy-start | bytes 13828
  6.5 4.3 %copy-start.13 = (s32[1,192]{1,0:T(1,128)S(1)}, s32[1,192]{1,0:T(1,128)}, u32[]{:S(2)}) copy-start(s32[1,192]{1,0:T(1,128)} %param.20) | copy-start | bytes 2308
  6.5 14.1 %copy-start.4 = (bf16[72,1152]{1,0:T(8,128)(2,1)S(1)}, bf16[72,1152]{1,0:T(8,128)(2,1)}, u32[]{:S(2)}) copy-start(bf16[72,1152]{1,0:T(8,128)(2,1)} %param.28) | copy-start | bytes 497668
  6.5 104.1 %all-gather.4.cloned.1.call-start = ((), (), s32[]{:S(2)}) async-start(), calls=%async_computation.4 | async-start | bytes 7520256 | tf_op jit(solution)/shard_map/all_gather | solution.py:107
  6.6 3.2 %copy-start.7 = (f32[1152]{0:T(1024)S(1)}, f32[1152]{0:T(1024)}, u32[]{:S(2)}) copy-start(f32[1152]{0:T(1024)} %param.25) | copy-start | bytes 13828
  11.5 31.2 %all-to-all-start = ((s32[16,1,192]{2,1,0:T(1,128)}), s32[16,1,192]{2,1,0:T(1,128)}, u32[]{:S(2)}, u32[]{:S(2)}) async-start(s32[16,1,192]{2,1,0:T(1,128)} %broadcast_in_dim.24), calls=%async_computation | async-start | bytes 32768 | tf_op jit(solution)/shard_map/all_to_all | solution.py:15
  20.6 148.7 %all-gather.6.cloned.1.call-start = ((), (), s32[]{:S(2)}) async-start(), calls=%async_computation.5 | async-start | bytes 3317760 | tf_op jit(solution)/shard_map/all_gather | solution.py:34
  44.3 71.9 %copy-start.5 = (s32[16,1,192]{2,0,1:T(8,128)}, s32[16,1,192]{2,0,1:T(8,128)S(1)}, u32[]{:S(2)}) copy-start(s32[16,1,192]{2,0,1:T(8,128)S(1)} %copy.41) | copy-start | bytes 36868
  126.2 1.2 copy-start.3
  132.0 1.1 copy-start.3
  137.7 1.1 copy-start.3
  143.3 1.2 copy-start.3
  149.0 1.1 copy-start.3
  154.7 1.1 copy-start.3
  157.9 11.3 %copy-start.10 = (bf16[1152]{0:T(1024)(128)(2,1)S(1)}, bf16[1152]{0:T(1024)(128)(2,1)}, u32[]{:S(2)}) copy-start(bf16[1152]{0:T(1024)(128)(2,1)} %param.29) | copy-start | bytes 6916
  164.5 16.6 %all-to-all-start.1 = ((bf16[16,192,72]{1,2,0:T(8,128)(2,1)}), bf16[16,192,72]{1,2,0:T(8,128)(2,1)}, u32[]{:S(2)}, u32[]{:S(2)}) async-start(bf16[16,192,72]{1,2,0:T(8,128)(2,1)} %copy.36), calls=%async_computation.1 | async-start | bytes 1179648 | tf_op jit(solution)/shard_map/all_to_all | solution.py:113
  172.8 12.0 %copy-start.8 = (f32[1152]{0:T(1024)S(1)}, f32[1152]{0:T(1024)}, u32[]{:S(2)}) copy-start(f32[1152]{0:T(1024)} %param.31) | copy-start | bytes 13828
  172.8 12.0 %copy-start.9 = (f32[1152]{0:T(1024)S(1)}, f32[1152]{0:T(1024)}, u32[]{:S(2)}) copy-start(f32[1152]{0:T(1024)} %param.30) | copy-start | bytes 13828
  183.9 0.9 copy-start.1
  184.8 14.3 %copy-start.11 = (bf16[1076]{0:T(1024)(128)(2,1)S(1)}, bf16[1076]{0:T(1024)(128)(2,1)}, u32[]{:S(2)}) copy-start(bf16[1076]{0:T(1024)(128)(2,1)} %param.33) | copy-start | bytes 6460
  186.4 46.4 %all-to-all-start.2 = ((bf16[4,192,1152]{2,1,0:T(8,128)(2,1)}), bf16[4,192,1152]{2,1,0:T(8,128)(2,1)}, u32[]{:S(2)}, u32[]{:S(2)}) async-start(bf16[4,192,1152]{2,1,0:T(8,128)(2,1)} %broadcast_in_dim.26), calls=%async_computation.2 | async-start | bytes 3538944 | tf_op jit(solution)/shard_map/all_to_all | solution.py:15
  199.1 106.7 %reduce-scatter.2.cloned.1.call-start = ((), (), s32[]{:S(2)}) async-start(), calls=%async_computation.6 | async-start | bytes 2211840 | tf_op jit(solution)/shard_map/reduce_scatter | solution.py:123
  232.8 13.3 %copy-start.12 = (bf16[1152]{0:T(1024)(128)(2,1)S(1)}, bf16[1152]{0:T(1024)(128)(2,1)}, u32[]{:S(2)}) copy-start(bf16[1152]{0:T(1024)(128)(2,1)} %param.35) | copy-start | bytes 6916
  232.8 73.0 %copy-start.2 = (f32[192,1152]{1,0:T(8,128)S(1)}, f32[192,1152]{1,0:T(8,128)}, u32[]{:S(2)}) copy-start(f32[192,1152]{1,0:T(8,128)} %copy-done.1) | copy-start | bytes 2654212
Sparse Core Ops, SparseCore 0:
  11.0 99.6 all-gather.3
  112.5 41.4 all-gather.5
  246.2 59.5 reduce-scatter.1
where the time goes:
time: 315 us; the launch traced here: 314 us
  waiting for transfers between devices  168 us (53%)
  matrix products  51.7 us (16%)
  starting transfers between devices  26.7 us (8%)
  local copies, waits for them, and re-layouts  22.1 us (7%)
  blocking collectives  22 us (7%)
  between operations  13.3 us (4%)
  other arithmetic  10.3 us (3%)
    all_gather x1, waiting for transfers between devices, per_device(): lax.all_gather(normed, SEQ, axis=0, tiled=True)  66.3 us
    reduce_scatter x1, waiting for transfers between devices, per_device(): lax.psum_scatter(jnp.dot(hidden, w_fc2, preferred_element_type=jnp.float3...  59.7 us
    all_to_all x2, waiting for transfers between devices, sent_to_all(): lax.all_to_all(jnp.broadcast_to(value[None], (size, *value.shape)), axis,...  33.6 us
    all_gather x1, blocking collectives, all_blocks(): blocks = lax.all_gather(blocks, axes[k], axis=0, tiled=True)  22 us
    all_to_all x2, starting transfers between devices, sent_to_all(): lax.all_to_all(jnp.broadcast_to(value[None], (size, *value.shape)), axis,...  21.8 us
    dot_general x6, matrix products, one_block(): lax.dot_general(rows, keys, (((1,), (1,)), ((), ())), preferred_element_t...  14.4 us
    dot_general x1, matrix products, per_device(): jnp.dot(hidden, w_fc2, preferred_element_type=jnp.float32)  13.3 us
    dot_general x6, matrix products, one_block(): jnp.dot(probs, value, preferred_element_type=jnp.float32)  12.7 us
  transfers between devices with their start and end apart: 6, of which 4 were waited for; matrix products, arithmetic and copies ran while one was open for 18% of the time, Pallas kernels for 0%

commit v1 on v0

v1 whole, which is shorter than its diff:
```python
import math

import jax
import jax.numpy as jnp
from jax import lax
from jax.experimental import pallas as pl
from jax.experimental.pallas import tpu as pltpu
from jax.sharding import Mesh
from jax.sharding import PartitionSpec as P

AXES = ("zl", "x", "y", "zh", "c")
SEQ = ("zl", "x")
BATCH = ("y", "zh", "c")
MESH_ID = pl.DeviceIdType.MESH
TOK = 192
WIDTH = 1152
ROW = 4 * TOK
HEAD = 72
WINDOW = 9 * TOK
QROWS = 224
OROWS = 96
F32 = jnp.float32
BF16 = jnp.bfloat16
NT = (((1,), (1,)), ((), ()))


def norm_rows(values, gain, shift):
    center = jnp.mean(values, -1, keepdims=True)
    moved = values - center
    spread = jnp.mean(jnp.square(moved), -1, keepdims=True)
    return moved * lax.rsqrt(spread + 1e-06) * gain + shift


def gelu(u):
    return 0.5 * u * (1.0 + jnp.tanh(math.sqrt(2.0 / math.pi) * (u + 0.044715 * u * u * u)))


def layer_kernel(
    patches,
    ints,
    rows_tab,
    cols_tab,
    vecs,
    w_a,
    w_b,
    w_f,
    out,
    emb,
    nrm,
    segs,
    seg_keys,
    seg_query,
    wz,
    wb,
    wp,
    wo,
    qs,
    kv,
    part_out,
    part_in,
    own_part,
    f_own,
    f_far,
    vecs_far,
    n2,
    hid,
    mlp,
    mlp_out,
    mlp_in,
    loc_sem,
    a_send,
    a_recv,
    as_send,
    as_recv,
    b_send,
    b_recv,
    bs_send,
    bs_recv,
    n_send,
    n_recv,
    s_send,
    s_recv,
    k_send,
    k_recv,
    f_send,
    f_recv,
    fx_send,
    fx_recv,
    fy_send,
    fy_recv,
    r_send,
    r_recv,
    m_send,
    m_recv,
):
    zl, x, y, zh, c = (lax.axis_index(a) for a in AXES)
    z = zh * 4 + zl

    def device(dz=0, dx=0, dy=0, dc=0, mirror=False):
        zz = 7 - z if mirror else lax.rem(z + dz + 8, 8)
        return {
            "zl": lax.rem(zz, 4),
            "x": lax.rem(x + dx + 4, 4),
            "y": lax.rem(y + dy + 4, 4),
            "zh": zz // 4,
            "c": lax.rem(c + dc, 2),
        }

    def remote(src, dst, send, recv, **where):
        return pltpu.make_async_remote_copy(
            src_ref=src,
            dst_ref=dst,
            send_sem=send,
            recv_sem=recv,
            device_id=device(**where),
            device_id_type=MESH_ID,
        )

    def around(v, d):
        return lax.rem(v + d + 4, 4)

    has_prev = zl > 0
    has_next = zl < 3

    barrier = pltpu.get_barrier_semaphore()
    peers = (
        [dict(dz=d) for d in (1, -1, 2, -2)]
        + [dict(dx=d) for d in (1, -1, 2)]
        + [dict(dy=d) for d in (1, -1, 2)]
        + [dict(dc=1), dict(mirror=True)]
    )
    for peer in peers:
        pl.semaphore_signal(barrier, inc=1, device_id=device(**peer), device_id_type=MESH_ID)
    pl.semaphore_wait(barrier, len(peers))

    local_a = pltpu.make_async_copy(w_a, wz.at[zl], loc_sem.at[0])
    local_b = pltpu.make_async_copy(w_b, wb.at[zl], loc_sem.at[1])
    local_f = pltpu.make_async_copy(w_f, f_own, loc_sem.at[2])
    local_a.start()

    def slab(src, dst, first, rows, send, recv, k, dz):
        at = pl.ds(pl.multiple_of(first, 16), rows)
        return remote(src.at[at], dst.at[zl, at], send.at[k], recv.at[k], dz=dz)

    half_a = c * (QROWS // 2)
    copies_a = [
        slab(w_a, wz, half_a, 112, a_send, a_recv, 0, 1),
        slab(w_a, wz, half_a, 112, a_send, a_recv, 1, -1),
        slab(w_a, wz, half_a, 64, a_send, a_recv, 2, 2),
        slab(w_a, wz, half_a + 64, 48, a_send, a_recv, 3, -2),
    ]
    for copy in copies_a:
        copy.start()
    local_b.start()
    local_f.start()

    ints_f = ints[...].astype(F32)
    level = lax.broadcasted_iota(jnp.int32, (128, 256), 0).astype(F32)
    wanted = jnp.where(level < 64.0, ints_f[1:2, :], ints_f[2:3, :] + 64.0)
    hot = jnp.transpose(jnp.where(level == wanted, 1.0, 0.0))[:TOK].astype(BF16)
    tables = jnp.concatenate([rows_tab[...], cols_tab[...]], axis=0)
    embedded = patches[...].astype(F32) + jnp.dot(hot, tables, preferred_element_type=F32)
    emb[...] = embedded
    nrm[x] = norm_rows(embedded, vecs[0:1, :], vecs[1:2, :]).astype(BF16)
    segs[1, x] = jnp.broadcast_to(ints_f[0:1, :], (8, 256))

    copies_n = []
    copies_s = []
    for k, dx in enumerate((1, -1, 2)):
        copies_n.append(remote(nrm.at[x], nrm.at[x], n_send.at[k], n_recv.at[k], dx=dx))
        copies_s.append(
            remote(segs.at[1, x], segs.at[1, x], s_send.at[k], s_recv.at[k], dx=dx)
        )
    for copy in copies_s + copies_n:
        copy.start()

    wp[...] = jnp.zeros_like(wp)
    wo[...] = jnp.zeros_like(wo)

    @pl.when(jnp.logical_not(has_prev))
    def _():
        kv[0:ROW, :] = jnp.zeros((ROW, 640), BF16)
        segs[0] = jnp.full((4, 8, 256), -1.0, F32)

    @pl.when(jnp.logical_not(has_next))
    def _():
        kv[2 * ROW : 3 * ROW, :] = jnp.zeros((ROW, 640), BF16)
        segs[2] = jnp.full((4, 8, 256), -1.0, F32)

    def to_sibling(buf, first, rows, send, recv):
        at = pl.ds(pl.multiple_of(first, 16), rows)
        made = []
        for k, d in enumerate((-1, 1, 2)):
            ref = buf.at[around(zl, d), at]
            made.append(remote(ref, ref, send.at[k], recv.at[k], dc=1))
        return made

    copies_as = to_sibling(wz, half_a, QROWS // 2, as_send, as_recv)
    for copy in copies_a:
        copy.wait_recv()
    for copy in copies_as:
        copy.start()

    def piece(px):
        return pl.ds(pl.multiple_of((y * 4 + px) * 144, 16), 144)

    cross = remote(w_f.at[piece(x)], f_far.at[piece(x)], f_send.at[0], f_recv.at[0], mirror=True)
    cross_v = remote(vecs, vecs_far, f_send.at[1], f_recv.at[1], mirror=True)
    cross.start()
    cross_v.start()

    local_a.wait()
    for copy in copies_as:
        copy.wait_recv()
    for h in range(4):
        wp[144 * h : 144 * h + 80, :] = wz[h, 0:80, :]
        wp[512 + 144 * h : 656 + 144 * h, :] = wz[h, 80:QROWS, :]

    copies_k = []

    def project(k, source):
        tokens = nrm[source]
        at = pl.ds(pl.multiple_of(source * TOK, TOK), TOK)
        qs[at, :] = lax.dot_general(
            tokens, wp[0:512, :], NT, preferred_element_type=F32
        ).astype(BF16)
        here = pl.ds(pl.multiple_of(ROW + source * TOK, TOK), TOK)
        kv[here, :] = lax.dot_general(
            tokens, wp[512:1152, :], NT, preferred_element_type=F32
        ).astype(BF16)
        as_next = pl.ds(pl.multiple_of(2 * ROW + source * TOK, TOK), TOK)
        up = remote(kv.at[here], kv.at[at], k_send.at[0, k], k_recv.at[0, k], dz=1)
        down = remote(kv.at[here], kv.at[as_next], k_send.at[1, k], k_recv.at[1, k], dz=-1)
        copies_k.append((up, down))
        pl.when(has_next)(up.start)
        pl.when(has_prev)(down.start)

    project(0, x)
    for k, dx in enumerate((-1, 1, 2)):
        copies_n[k].wait_recv()
        project(k + 1, around(x, dx))
    for copy in copies_s:
        copy.wait_recv()
    seg_up = remote(segs.at[1], segs.at[0], s_send.at[3], s_recv.at[3], dz=1)
    seg_down = remote(segs.at[1], segs.at[2], s_send.at[4], s_recv.at[4], dz=-1)
    pl.when(has_next)(seg_up.start)
    pl.when(has_prev)(seg_down.start)

    half_b = c * (OROWS // 2)
    copies_b = [
        slab(w_b, wb, half_b, 48, b_send, b_recv, 0, 1),
        slab(w_b, wb, half_b, 48, b_send, b_recv, 1, -1),
        slab(w_b, wb, half_b, 32, b_send, b_recv, 2, 2),
        slab(w_b, wb, half_b + 32, 16, b_send, b_recv, 3, -2),
    ]
    for copy in copies_b:
        copy.start()

    copies_fx = []
    copies_fy = []

    def share_y(k, px):
        made = [
            remote(f_far.at[piece(px)], f_far.at[piece(px)], fy_send.at[k, i], fy_recv.at[k, i], dy=dy)
            for i, dy in enumerate((1, -1, 2))
        ]
        for copy in made:
            copy.start()
        copies_fy.extend(made)

    cross.wait_recv()
    for k, dx in enumerate((1, -1, 2)):
        copy = remote(f_far.at[piece(x)], f_far.at[piece(x)], fx_send.at[k], fx_recv.at[k], dx=dx)
        copy.start()
        copies_fx.append(copy)
    share_y(0, x)

    copies_bs = to_sibling(wb, half_b, OROWS // 2, bs_send, bs_recv)
    for copy in copies_b:
        copy.wait_recv()
    for copy in copies_bs:
        copy.start()
    for k, dx in enumerate((-1, 1, 2)):
        copies_fx[k].wait_recv()
        share_y(k + 1, around(x, dx))
    local_b.wait()
    for copy in copies_bs:
        copy.wait_recv()
    for h in range(4):
        wo[h, 16 * h + 64 : 16 * h + 64 + OROWS, :] = wb[h]

    pl.when(has_prev)(seg_up.wait_recv)
    pl.when(has_next)(seg_down.wait_recv)
    for j in range(4):
        parts = [segs[b // 4, b % 4][:, :TOK] for b in range(j, j + 9)]
        seg_keys[j] = jnp.concatenate(parts, axis=1)
        mine = segs[1, j]
        spread = jnp.concatenate([mine] * 16, axis=0)
        seg_query[j] = jnp.transpose(spread)[:TOK]

    for up, down in copies_k:
        pl.when(has_prev)(up.wait_recv)
        pl.when(has_next)(down.wait_recv)

    scale = 1.0 / math.sqrt(HEAD)

    def attend(j):
        at = pl.ds(pl.multiple_of(j * TOK, TOK), TOK)
        window = pl.ds(pl.multiple_of(j * TOK, TOK), WINDOW)
        same = seg_query[j][:, 0:1] == seg_keys[j][0:1, :]
        total = None
        for h in range(4):
            scores = lax.dot_general(
                qs[at, 128 * h : 128 * h + 128],
                kv[window, 128 * h : 128 * h + 128],
                NT,
                preferred_element_type=F32,
            )
            scores = jnp.where(same, scores, -jnp.inf)
            top = jnp.max(scores, -1, keepdims=True)
            expo = jnp.exp((scores - top) * scale)
            weight = jnp.sum(expo, -1, keepdims=True)
            mixed = jnp.dot(
                expo.astype(BF16), kv[window, 128 * h : 128 * h + 256], preferred_element_type=F32
            )
            mixed = (mixed / weight).astype(BF16)
            term = jnp.dot(mixed, wo[h], preferred_element_type=F32)
            total = term if total is None else total + term
        return total

    def send_part(k, px):
        return pltpu.make_async_remote_copy(
            src_ref=part_out.at[k],
            dst_ref=part_in.at[k],
            send_sem=r_send.at[k],
            recv_sem=r_recv.at[k],
            device_id={"zl": zl, "x": px, "y": y, "zh": zh, "c": c},
            device_id_type=MESH_ID,
        )

    def attend_step(k, carry):
        j = around(x, k + 1)
        total = attend(j)

        @pl.when(k < 3)
        def _():
            part_out[k] = total.astype(BF16)
            send_part(k, j).start()

        @pl.when(k == 3)
        def _():
            own_part[...] = total

        return carry

    lax.fori_loop(0, 4, attend_step, 0)

    attended = emb[...] + own_part[...] + vecs[4:5, :]
    for k in range(3):
        send_part(k, around(x, k + 1)).wait_recv()
        attended = attended + part_in[k].astype(F32)
    own_part[...] = attended
    n2[c] = norm_rows(attended, vecs[2:3, :], vecs[3:4, :]).astype(BF16)
    give = remote(n2.at[c], n2.at[c], m_send.at[0], m_recv.at[0], dc=1)
    give.start()
    local_f.wait()
    give.wait_recv()

    tokens = n2[...].reshape(2 * TOK, WIDTH)

    def hidden_of(weights, biases):
        def step(i, carry):
            at = pl.ds(pl.multiple_of(i * 384, 384), 384)
            inner = jnp.dot(tokens, weights[0:WIDTH, at], preferred_element_type=F32)
            hid[:, at] = gelu(inner + biases[6:7, at]).astype(BF16)
            return carry

        lax.fori_loop(0, 3, step, 0)

    def project_hidden(weights, first):
        def step(i, carry):
            at = pl.ds(pl.multiple_of(i * 384, 384), 384)
            got = jnp.dot(hid[...], weights[WIDTH : 2 * WIDTH, at], preferred_element_type=F32)
            mlp[:, at] = got if first else mlp[:, at] + got
            return carry

        lax.fori_loop(0, 3, step, 0)

    hidden_of(f_own, vecs)
    project_hidden(f_own, True)
    for copy in copies_fy:
        copy.wait_recv()
    cross_v.wait_recv()
    hidden_of(f_far, vecs_far)
    project_hidden(f_far, False)

    mine_at = pl.ds(pl.multiple_of(c * TOK, TOK), TOK)
    other_at = pl.ds(pl.multiple_of((1 - c) * TOK, TOK), TOK)
    mlp_out[...] = mlp[other_at, :].astype(BF16)
    back = remote(mlp_out, mlp_in, m_send.at[1], m_recv.at[1], dc=1)
    back.start()
    mine_sum = own_part[...] + vecs[5:6, :] + mlp[mine_at, :]
    back.wait_recv()
    out[...] = (mine_sum + mlp_in[...].astype(F32)).astype(BF16)

    for copy in copies_a + copies_as + copies_n + copies_s + copies_b + copies_bs:
        copy.wait_send()
    for up, down in copies_k:
        pl.when(has_next)(up.wait_send)
        pl.when(has_prev)(down.wait_send)
    pl.when(has_next)(seg_up.wait_send)
    pl.when(has_prev)(seg_down.wait_send)
    for copy in [cross, cross_v, give, back] + copies_fx + copies_fy:
        copy.wait_send()
    for k in range(3):
        send_part(k, around(x, k + 1)).wait_send()


def layer_call(*operands):
    vmem = pl.BlockSpec(memory_space=pltpu.VMEM)
    hbm = pl.BlockSpec(memory_space=pl.ANY)
    dma = pltpu.SemaphoreType.DMA
    scratch = [
        pltpu.VMEM((TOK, WIDTH), F32),
        pltpu.VMEM((4, TOK, WIDTH), BF16),
        pltpu.VMEM((3, 4, 8, 256), F32),
        pltpu.VMEM((4, 8, WINDOW), F32),
        pltpu.VMEM((4, TOK, 128), F32),
        pltpu.VMEM((4, QROWS, WIDTH), BF16),
        pltpu.VMEM((4, OROWS, WIDTH), BF16),
        pltpu.VMEM((WIDTH, WIDTH), BF16),
        pltpu.VMEM((4, 256, WIDTH), BF16),
        pltpu.VMEM((ROW, 512), BF16),
        pltpu.VMEM((3 * ROW, 640), BF16),
        pltpu.VMEM((3, TOK, WIDTH), BF16),
        pltpu.VMEM((3, TOK, WIDTH), BF16),
        pltpu.VMEM((TOK, WIDTH), F32),
        pltpu.VMEM((2 * WIDTH, WIDTH), BF16),
        pltpu.VMEM((2 * WIDTH, WIDTH), BF16),
        pltpu.VMEM((8, WIDTH), F32),
        pltpu.VMEM((2, TOK, WIDTH), BF16),
        pltpu.VMEM((2 * TOK, WIDTH), BF16),
        pltpu.VMEM((2 * TOK, WIDTH), F32),
        pltpu.VMEM((TOK, WIDTH), BF16),
        pltpu.VMEM((TOK, WIDTH), BF16),
        dma((3,)),
    ]
    for shape in ((4,), (3,), (4,), (3,), (3,), (5,), (2, 4), (2,), (3,), (4, 3), (3,), (2,)):
        scratch += [dma(shape), dma(shape)]
    return pl.pallas_call(
        layer_kernel,
        out_shape=jax.ShapeDtypeStruct((TOK, WIDTH), BF16),
        in_specs=[vmem] * 5 + [hbm] * 3,
        out_specs=vmem,
        scratch_shapes=scratch,
        compiler_params=pltpu.CompilerParams(
            collective_id=0, has_side_effects=True, vmem_limit_bytes=60 << 20
        ),
        name="encoder_layer",
    )(*operands)


def per_device(
    patches,
    seg_ids,
    pos_rows,
    pos_cols,
    row_table,
    col_table,
    ln1_gain,
    ln1_bias,
    w_qkv,
    w_out,
    out_bias,
    ln2_gain,
    ln2_bias,
    w_fc1,
    fc1_bias,
    w_fc2,
    fc2_bias,
):
    ints = jnp.pad(jnp.concatenate([seg_ids, pos_rows, pos_cols], 0), ((0, 5), (0, 64)))
    pad_hidden = WIDTH - w_fc1.shape[1]
    vecs = jnp.stack(
        [
            ln1_gain,
            ln1_bias,
            ln2_gain,
            ln2_bias,
            out_bias.astype(F32),
            fc2_bias.astype(F32),
            jnp.pad(fc1_bias.astype(F32), (0, pad_hidden)),
            jnp.zeros_like(ln1_gain),
        ]
    )
    turned = w_qkv.T
    w_a = jnp.concatenate(
        [turned[:HEAD], jnp.zeros((8, WIDTH), BF16), turned[HEAD:]], axis=0
    )
    w_b = jnp.pad(w_out, ((8, OROWS - HEAD - 8), (0, 0)))
    w_f = jnp.concatenate(
        [jnp.pad(w_fc1, ((0, 0), (0, pad_hidden))), jnp.pad(w_fc2, ((0, pad_hidden), (0, 0)))],
        axis=0,
    )
    return layer_call(patches[0], ints, row_table, col_table, vecs, w_a, w_b, w_f)[None]


def solution(mesh):
    torus = Mesh(mesh.devices.reshape(4, 4, 4, 2, 2), AXES)
    in_specs = (
        P(BATCH, SEQ, None),
        P(BATCH, SEQ),
        P(BATCH, SEQ),
        P(BATCH, SEQ),
        P(),
        P(),
        P(),
        P(),
        P(None, SEQ),
        P(SEQ, None),
        P(),
        P(),
        P(),
        P(None, ("zh", "c")),
        P(("zh", "c")),
        P(("zh", "c"), None),
        P(),
    )
    return jax.shard_map(
        per_device,
        mesh=torus,
        in_specs=in_specs,
        out_specs=P(BATCH, SEQ, None),
        check_vma=False,
    )
```

time: 315 us -> 130 us (0.41)
  waiting for transfers between devices: 168 us -> 0 us
  Pallas kernels: 0 us -> 113 us
  matrix products: 51.7 us -> 0 us
  starting transfers between devices: 26.7 us -> 0 us
  blocking collectives: 22 us -> 0 us
  between operations: 13.3 us -> 0.23 us
  local copies, waits for them, and re-layouts: 22.1 us -> 9.99 us
  other arithmetic: 10.3 us -> 6.61 us
    pallas_call x0 -> x1, Pallas kernels: none -> 113 us  [layer_call(): pl.pallas_call(layer_kernel, out_shape=jax.ShapeDtypeStruct((TOK, WIDTH),...]
    all_gather x2 -> x0, waiting for transfers between devices: 66.4 us -> none  [the longest x1 66.3 us: per_device(): lax.all_gather(normed, SEQ, axis=0, tiled=True)]
    reduce_scatter x1 -> x0, waiting for transfers between devices: 59.7 us -> none  [per_device(): lax.psum_scatter(jnp.dot(hidden, w_fc2, preferred_element_type=jnp.float3...]
    dot_general x17 -> x0, matrix products: 51.7 us -> none  [the longest x6 14.4 us: one_block(): lax.dot_general(rows, keys, (((1,), (1,)), ((), ())), preferred_element_t...]
    all_to_all x3 -> x0, waiting for transfers between devices: 41.9 us -> none  [the longest x2 33.6 us: sent_to_all(): lax.all_to_all(jnp.broadcast_to(value[None], (size, *value.shape)), axis,...]
    all_to_all x3 -> x0, starting transfers between devices: 26.6 us -> none  [the longest x2 21.8 us: sent_to_all(): lax.all_to_all(jnp.broadcast_to(value[None], (size, *value.shape)), axis,...]
    all_gather x1 -> x0, blocking collectives: 22 us -> none  [all_blocks(): blocks = lax.all_gather(blocks, axes[k], axis=0, tiled=True)]
    while x16 -> x0, local copies, waits for them, and re-layouts: 9.43 us -> none  [the longest x4 8.52 us: attend_head(): return lax.map(one_block, (query, seg_query)).reshape(length, head_dim)]
  transfers between devices with their start and end apart: 6 -> 0, of which waited for: 4 -> 0; matrix products, arithmetic and copies ran while one was open for 18% -> 0% of each run, Pallas kernels for 0% -> 0%
where the time goes in v1:
time: 130 us; the launch traced here: 129 us
  Pallas kernels  113 us (87%)
  local copies, waits for them, and re-layouts  9.99 us (8%)
  other arithmetic  6.61 us (5%)
    pallas_call x1, Pallas kernels, layer_call(): pl.pallas_call(layer_kernel, out_shape=jax.ShapeDtypeStruct((TOK, WIDTH),...  113 us
    unnamed x24, local copies, waits for them, and re-layouts  5.95 us
    concatenate x1, other arithmetic, per_device(): jnp.concatenate([jnp.pad(w_fc1, ((0, 0), (0, pad_hidden))), jnp.pad(w_fc2...  5.6 us

profile of v1, /device:TPU:1, one launch (start us, length us, event | category | flops | bytes accessed | tf_op | source)
XLA Modules:
  0.0 129.4 jit_solution(11704508407102543248)
XLA Ops:
  0.0 1.0 slice.9
  1.0 0.9 slice.8
  1.9 0.1 pad.29.clone
  2.0 1.0 pad_maximum_fusion.w_a
  3.0 4.1 %copy.18 = bf16[1152,1076]{1,0:T(8,128)(2,1)S(1)} copy(bf16[1152,1076]{0,1:T(8,128)(2,1)} %param.30) | data formatting | bytes 4958208 | tf_op args[13]
  7.1 0.0 copy-start
  7.1 0.0 copy-start.5
  7.1 0.0 copy-start.6
  7.1 0.0 copy-start.7
  7.1 0.0 copy-start.1
  7.2 0.0 copy-start.2
  7.2 0.0 copy-start.3
  7.2 0.0 copy-start.4
  7.2 0.0 copy-start.8
  7.2 0.0 copy-start.9
  7.2 0.0 copy-start.10
  7.2 5.6 %fusion.2.w_f = bf16[2304,1152]{1,0:T(8,128)(2,1)} fusion(bf16[1076,1152]{1,0:T(8,128)(2,1)} %param.32, bf16[1152,1076]{1,0:T(8,128)(2,1)S(1)} %copy.18), kind=kLoop, calls=%fused_computation.4 | loop fusion | flops 21233664 | bytes 10266624 | tf_op jit(solution)/shard_map/concatenate | solution.py:501
  12.8 0.0 copy-done
  12.8 0.7 pad.23.w_b
  13.5 0.0 copy-done.5
  13.6 0.0 copy-done.6
  13.6 0.0 copy-done.7
  13.6 0.0 copy-done.1
  13.6 0.0 copy-done.2
  13.6 0.0 copy-done.3
  13.7 0.0 copy-done.4
  13.7 0.7 stack.43.vecs
  14.4 0.0 copy-done.8
  14.4 0.0 copy-done.9
  14.4 0.6 pad.21.ints
  15.0 112.5 %encoder_layer.1 = bf16[192,1152]{1,0:T(8,128)(2,1)} custom-call(bf16[192,1152]{1,0:T(8,128)(2,1)} %bitcast.6, s32[8,256]{1,0:T(8,128)} %pad.21.ints, bf16[64,1152]{1,0:T(8,128)(2,1)} %rows_tab.1, bf16[64,1152]{1,0:T(8,128)(2,1)} %cols_tab.1, f32[8,1152]{1,0:T(8,128)} %stack.43.vecs, bf16[224,1152]{1,0:T(8,128)(2,1)} %pad_maximum_fusion.w_a, ...), custom_call_target="tpu_custom_call" | custom-call | tf_op jit(solution)/shard_map/encoder_layer/pallas_call | solution.py:450
  127.6 1.8 %copy.20 = bf16[1,192,1152]{2,1,0:T(8,128)(2,1)} copy(bf16[1,192,1152]{2,1,0:T(8,128)(2,1)} %bitcast.3) | data formatting | bytes 884736
  (12 shorter events, 0.1 us)
Async XLA Ops:
  7.1 5.7 %copy-start = (bf16[72,1152]{1,0:T(8,128)(2,1)S(1)}, bf16[72,1152]{1,0:T(8,128)(2,1)}, u32[]{:S(2)}) copy-start(bf16[72,1152]{1,0:T(8,128)(2,1)} %param.26) | copy-start | bytes 497668
  7.1 6.4 %copy-start.5 = (bf16[1076]{0:T(1024)(128)(2,1)S(1)}, bf16[1076]{0:T(1024)(128)(2,1)}, u32[]{:S(2)}) copy-start(bf16[1076]{0:T(1024)(128)(2,1)} %param.31) | copy-start | bytes 6460
  7.1 6.4 %copy-start.6 = (bf16[1152]{0:T(1024)(128)(2,1)S(1)}, bf16[1152]{0:T(1024)(128)(2,1)}, u32[]{:S(2)}) copy-start(bf16[1152]{0:T(1024)(128)(2,1)} %param.27) | copy-start | bytes 6916
  7.1 6.4 %copy-start.7 = (bf16[1152]{0:T(1024)(128)(2,1)S(1)}, bf16[1152]{0:T(1024)(128)(2,1)}, u32[]{:S(2)}) copy-start(bf16[1152]{0:T(1024)(128)(2,1)} %param.33) | copy-start | bytes 6916
  7.1 6.5 %copy-start.1 = (f32[1152]{0:T(1024)S(1)}, f32[1152]{0:T(1024)}, u32[]{:S(2)}) copy-start(f32[1152]{0:T(1024)} %param.23) | copy-start | bytes 13828
  7.2 6.5 %copy-start.2 = (f32[1152]{0:T(1024)S(1)}, f32[1152]{0:T(1024)}, u32[]{:S(2)}) copy-start(f32[1152]{0:T(1024)} %param.24) | copy-start | bytes 13828
  7.2 6.5 %copy-start.3 = (f32[1152]{0:T(1024)S(1)}, f32[1152]{0:T(1024)}, u32[]{:S(2)}) copy-start(f32[1152]{0:T(1024)} %param.28) | copy-start | bytes 13828
  7.2 6.5 %copy-start.4 = (f32[1152]{0:T(1024)S(1)}, f32[1152]{0:T(1024)}, u32[]{:S(2)}) copy-start(f32[1152]{0:T(1024)} %param.29) | copy-start | bytes 13828
  7.2 7.2 %copy-start.8 = (s32[1,192]{1,0:T(1,128)S(1)}, s32[1,192]{1,0:T(1,128)}, u32[]{:S(2)}) copy-start(s32[1,192]{1,0:T(1,128)} %param.20) | copy-start | bytes 2308
  7.2 7.2 %copy-start.9 = (s32[1,192]{1,0:T(1,128)S(1)}, s32[1,192]{1,0:T(1,128)}, u32[]{:S(2)}) copy-start(s32[1,192]{1,0:T(1,128)} %param.19) | copy-start | bytes 2308
  7.2 7.2 %copy-start.10 = (s32[1,192]{1,0:T(1,128)S(1)}, s32[1,192]{1,0:T(1,128)}, u32[]{:S(2)}) copy-start(s32[1,192]{1,0:T(1,128)} %param.18) | copy-start | bytes 2308

commit v2 on v1

v2 whole, which is shorter than its diff:
```python
import math

import jax
import jax.numpy as jnp
from jax import lax
from jax.experimental import pallas as pl
from jax.experimental.pallas import tpu as pltpu
from jax.sharding import Mesh
from jax.sharding import PartitionSpec as P

AXES = ("zl", "x", "y", "zh", "c")
SEQ = ("zl", "x")
BATCH = ("y", "zh", "c")
MESH_ID = pl.DeviceIdType.MESH
TOK = 192
WIDTH = 1152
ROW = 4 * TOK
HEAD = 72
WINDOW = 9 * TOK
QROWS = 224
OROWS = 96
F32 = jnp.float32
BF16 = jnp.bfloat16
NT = (((1,), (1,)), ((), ()))


def norm_rows(values, gain, shift):
    center = jnp.mean(values, -1, keepdims=True)
    moved = values - center
    spread = jnp.mean(jnp.square(moved), -1, keepdims=True)
    return moved * lax.rsqrt(spread + 1e-06) * gain + shift


def gelu(u):
    return 0.5 * u * (1.0 + jnp.tanh(math.sqrt(2.0 / math.pi) * (u + 0.044715 * u * u * u)))


def layer_kernel(
    patches,
    seg_in,
    rows_in,
    cols_in,
    rows_tab,
    cols_tab,
    ln1_gain,
    ln1_bias,
    ln2_gain,
    ln2_bias,
    out_bias,
    fc2_bias,
    fc1_bias,
    w_a,
    w_b,
    w_1,
    w_2,
    w_tail,
    out,
    emb,
    nrm,
    segs,
    seg_keys,
    seg_query,
    wz,
    wb,
    wp,
    wo,
    qs,
    kv,
    part_out,
    part_in,
    own_part,
    f_own,
    f_far,
    bias_own,
    bias_far,
    stage_a,
    stage_b,
    ring_in,
    n2,
    hid,
    mlp,
    mlp_out,
    mlp_in,
    loc_sem,
    a_send,
    a_recv,
    as_send,
    as_recv,
    b_send,
    b_recv,
    bs_send,
    bs_recv,
    n_send,
    n_recv,
    s_send,
    s_recv,
    k_send,
    k_recv,
    f_send,
    f_recv,
    f1_send,
    f1_recv,
    f2_send,
    f2_recv,
    r_send,
    r_recv,
    m_send,
    m_recv,
):
    zl, x, y, zh, c = (lax.axis_index(a) for a in AXES)
    z = zh * 4 + zl

    def device(dz=0, dx=0, dy=0, dc=0, mirror=False):
        zz = 7 - z if mirror else lax.rem(z + dz + 8, 8)
        return {
            "zl": lax.rem(zz, 4),
            "x": lax.rem(x + dx + 4, 4),
            "y": lax.rem(y + dy + 4, 4),
            "zh": zz // 4,
            "c": lax.rem(c + dc, 2),
        }

    def remote(src, dst, send, recv, **where):
        return pltpu.make_async_remote_copy(
            src_ref=src,
            dst_ref=dst,
            send_sem=send,
            recv_sem=recv,
            device_id=device(**where),
            device_id_type=MESH_ID,
        )

    def around(v, d):
        return lax.rem(v + d + 4, 4)

    has_prev = zl > 0
    has_next = zl < 3

    barrier = pltpu.get_barrier_semaphore()
    peers = (
        [dict(dz=d) for d in (1, -1, 2, -2)]
        + [dict(dx=d) for d in (1, -1, 2)]
        + [dict(dy=d) for d in (1, -1, 2)]
        + [dict(dc=1), dict(mirror=True)]
    )
    for peer in peers:
        pl.semaphore_signal(barrier, inc=1, device_id=device(**peer), device_id_type=MESH_ID)

    local = [
        pltpu.make_async_copy(w_a, stage_a, loc_sem.at[0]),
        pltpu.make_async_copy(w_b, stage_b, loc_sem.at[1]),
        pltpu.make_async_copy(w_1.at[0:1024], f_own.at[0:1024], loc_sem.at[2]),
        pltpu.make_async_copy(w_2.at[0:1024], f_own.at[1152:2176], loc_sem.at[3]),
        pltpu.make_async_copy(w_tail.at[0:128], f_own.at[1024:1152], loc_sem.at[4]),
        pltpu.make_async_copy(w_tail.at[128:256], f_own.at[2176:2304], loc_sem.at[5]),
    ]
    for copy in local:
        copy.start()

    def wide(ref):
        return jnp.concatenate([ref[...].astype(F32), jnp.zeros((1, 64), F32)], axis=1)

    level = lax.broadcasted_iota(jnp.int32, (128, 256), 0).astype(F32)
    wanted = jnp.where(level < 64.0, wide(rows_in), wide(cols_in) + 64.0)
    hot = jnp.transpose(jnp.where(level == wanted, 1.0, 0.0))[:TOK].astype(BF16)
    tables = jnp.concatenate([rows_tab[...], cols_tab[...]], axis=0)
    embedded = patches[...].astype(F32) + jnp.dot(hot, tables, preferred_element_type=F32)
    emb[...] = embedded
    nrm[x] = norm_rows(embedded, ln1_gain[...], ln1_bias[...]).astype(BF16)
    segs[1, x] = jnp.broadcast_to(wide(seg_in), (8, 256))
    bias_own[...] = jnp.broadcast_to(fc1_bias[...], (8, WIDTH))

    local[0].wait()
    staged = stage_a[...].astype(F32)
    wz[zl] = jnp.concatenate(
        [staged[:HEAD], jnp.zeros((8, WIDTH), F32), staged[HEAD:]], axis=0
    ).astype(BF16)
    pl.semaphore_wait(barrier, len(peers))

    def slab(buf, first, rows, send, recv, k, dz):
        ref = buf.at[zl, pl.ds(pl.multiple_of(first, 16), rows)]
        return remote(ref, ref, send.at[k], recv.at[k], dz=dz)

    half_a = c * (QROWS // 2)
    copies_a = [
        slab(wz, half_a, 112, a_send, a_recv, 0, 1),
        slab(wz, half_a, 112, a_send, a_recv, 1, -1),
        slab(wz, half_a, 64, a_send, a_recv, 2, 2),
        slab(wz, half_a + 64, 48, a_send, a_recv, 3, -2),
    ]
    for copy in copies_a:
        copy.start()

    LOW, HIGH = pl.ds(0, 96), pl.ds(96, 96)
    copies_n = [
        remote(nrm.at[x], nrm.at[x], n_send.at[k], n_recv.at[k], dx=dx)
        for k, dx in enumerate((1, -1))
    ]
    copies_s = [
        remote(segs.at[1, x], segs.at[1, x], s_send.at[k], s_recv.at[k], dx=dx)
        for k, dx in enumerate((1, -1, 2))
    ]
    for copy in copies_n + copies_s:
        copy.start()

    def unit(py, px, first, rows):
        at = pl.multiple_of((py * 4 + px) * 144 + first, 16)
        return f_far.at[pl.ds(at, rows)]

    for copy in local[2:]:
        copy.wait()
    mine = pl.ds(pl.multiple_of((y * 4 + x) * 144, 16), 144)
    cross = remote(f_own.at[mine], f_far.at[mine], f_send.at[0], f_recv.at[0], mirror=True)
    cross_v = remote(bias_own, bias_far, f_send.at[1], f_recv.at[1], mirror=True)
    cross.start()
    cross_v.start()

    local[1].wait()
    wb[zl] = jnp.concatenate(
        [
            jnp.zeros((8, WIDTH), F32),
            stage_b[...].astype(F32),
            jnp.zeros((OROWS - HEAD - 8, WIDTH), F32),
        ],
        axis=0,
    ).astype(BF16)

    wp[...] = jnp.zeros_like(wp)
    wo[...] = jnp.zeros_like(wo)

    @pl.when(jnp.logical_not(has_prev))
    def _():
        kv[0:ROW, :] = jnp.zeros((ROW, 640), BF16)
        segs[0] = jnp.full((4, 8, 256), -1.0, F32)

    @pl.when(jnp.logical_not(has_next))
    def _():
        kv[2 * ROW : 3 * ROW, :] = jnp.zeros((ROW, 640), BF16)
        segs[2] = jnp.full((4, 8, 256), -1.0, F32)

    left, right, far_x = around(x, -1), around(x, 1), around(x, 2)
    copies_n[0].wait_recv()
    on_right = remote(nrm.at[left, LOW], nrm.at[left, LOW], n_send.at[2], n_recv.at[2], dx=1)
    on_right.start()
    copies_n[1].wait_recv()
    on_left = remote(nrm.at[right, HIGH], nrm.at[right, HIGH], n_send.at[3], n_recv.at[3], dx=-1)
    on_left.start()

    def to_sibling(buf, first, rows, send, recv):
        at = pl.ds(pl.multiple_of(first, 16), rows)
        made = []
        for k, d in enumerate((-1, 1, 2)):
            ref = buf.at[around(zl, d), at]
            made.append(remote(ref, ref, send.at[k], recv.at[k], dc=1))
        return made

    copies_as = to_sibling(wz, half_a, QROWS // 2, as_send, as_recv)
    for copy in copies_a:
        copy.wait_recv()
    for copy in copies_as:
        copy.start()
    for copy in copies_as:
        copy.wait_recv()
    for h in range(4):
        wp[144 * h : 144 * h + 80, :] = wz[h, 0:80, :]
        wp[512 + 144 * h : 656 + 144 * h, :] = wz[h, 80:QROWS, :]

    copies_k = []

    def project(k, source):
        tokens = nrm[source]
        at = pl.ds(pl.multiple_of(source * TOK, TOK), TOK)
        here = pl.ds(pl.multiple_of(ROW + source * TOK, TOK), TOK)
        as_next = pl.ds(pl.multiple_of(2 * ROW + source * TOK, TOK), TOK)
        kv[here, :] = lax.dot_general(
            tokens, wp[512:1152, :], NT, preferred_element_type=F32
        ).astype(BF16)
        up = remote(kv.at[here], kv.at[at], k_send.at[0, k], k_recv.at[0, k], dz=1)
        down = remote(kv.at[here], kv.at[as_next], k_send.at[1, k], k_recv.at[1, k], dz=-1)
        copies_k.append((up, down))
        pl.when(has_next)(up.start)
        pl.when(has_prev)(down.start)
        qs[at, :] = lax.dot_general(
            tokens, wp[0:512, :], NT, preferred_element_type=F32
        ).astype(BF16)

    project(0, x)
    project(1, left)
    project(2, right)

    PARTS = ((0, 80, 48), (80, 64, 32))
    def held(part, k, db=0):
        d = (0, -1, 1, 2)[k]
        if part == 0:
            return around(y, db), around(x, d)
        return around(y, d), around(x, db)

    def along(part, phase, d):
        return dict(dx=d) if (part == 0) == (phase == 0) else dict(dy=d)

    def first_copy(part, i):
        first, rows, _ = PARTS[part]
        ref = unit(y, x, first, rows)
        d = (1, -1, 2)[i]
        return remote(ref, ref, f1_send.at[part, i], f1_recv.at[part, i], **along(part, 0, d))

    def second_copy(part, k, i):
        first, rows, _ = PARTS[part]
        ref = unit(*held(part, k), first, rows)
        return remote(
            ref, ref, f2_send.at[part, k, i], f2_recv.at[part, k, i], **along(part, 1, (1, -1)[i])
        )

    def hand_copy(part, k, i):
        first, rows, half = PARTS[part]
        cut = ((first, half), (first + half, rows - half))[i]
        d = (1, -1)[i]
        ref = unit(*held(part, k, -d), *cut)
        at = (part, k, 2 + i)
        return remote(ref, ref, f2_send.at[at], f2_recv.at[at], **along(part, 1, d))

    def start_first(part):
        for i in range(3):
            first_copy(part, i).start()

    def start_second(part, k):
        for i in range(2):
            second_copy(part, k, i).start()

    def hand_on(part, k):
        for i in range(2):
            second_copy(part, k, i).wait_recv()
            hand_copy(part, k, i).start()

    cross.wait_recv()
    for part in (0, 1):
        start_first(part)
        start_second(part, 0)

    on_right.wait_recv()
    on_left.wait_recv()
    project(3, far_x)
    for copy in copies_s:
        copy.wait_recv()
    seg_up = remote(segs.at[1], segs.at[0], s_send.at[3], s_recv.at[3], dz=1)
    seg_down = remote(segs.at[1], segs.at[2], s_send.at[4], s_recv.at[4], dz=-1)
    pl.when(has_next)(seg_up.start)
    pl.when(has_prev)(seg_down.start)

    half_b = c * (OROWS // 2)
    copies_b = [
        slab(wb, half_b, 48, b_send, b_recv, 0, 1),
        slab(wb, half_b, 48, b_send, b_recv, 1, -1),
        slab(wb, half_b, 32, b_send, b_recv, 2, 2),
        slab(wb, half_b + 32, 16, b_send, b_recv, 3, -2),
    ]
    for copy in copies_b:
        copy.start()

    for k in (1, 2, 3):
        for part in (1, 0):
            first_copy(part, k - 1).wait_recv()
            start_second(part, k)
    for part in (1, 0):
        hand_on(part, 0)

    copies_bs = to_sibling(wb, half_b, OROWS // 2, bs_send, bs_recv)
    for copy in copies_b:
        copy.wait_recv()
    for copy in copies_bs:
        copy.start()

    pl.when(has_prev)(seg_up.wait_recv)
    pl.when(has_next)(seg_down.wait_recv)
    for j in range(4):
        parts = [segs[b // 4, b % 4][:, :TOK] for b in range(j, j + 9)]
        seg_keys[j] = jnp.concatenate(parts, axis=1)
        mine_seg = segs[1, j]
        spread = jnp.concatenate([mine_seg] * 16, axis=0)
        seg_query[j] = jnp.transpose(spread)[:TOK]
    for copy in copies_bs:
        copy.wait_recv()
    for h in range(4):
        wo[h, 16 * h + 64 : 16 * h + 64 + OROWS, :] = wb[h]

    for up, down in copies_k:
        pl.when(has_prev)(up.wait_recv)
        pl.when(has_next)(down.wait_recv)

    scale = 1.0 / math.sqrt(HEAD)

    def attend(j):
        at = pl.ds(pl.multiple_of(j * TOK, TOK), TOK)
        window = pl.ds(pl.multiple_of(j * TOK, TOK), WINDOW)
        same = seg_query[j][:, 0:1] == seg_keys[j][0:1, :]
        total = None
        for h in range(4):
            scores = lax.dot_general(
                qs[at, 128 * h : 128 * h + 128],
                kv[window, 128 * h : 128 * h + 128],
                NT,
                preferred_element_type=F32,
            )
            scores = jnp.where(same, scores, -jnp.inf)
            top = jnp.max(scores, -1, keepdims=True)
            expo = jnp.exp((scores - top) * scale)
            weight = jnp.sum(expo, -1, keepdims=True)
            mixed = jnp.dot(
                expo.astype(BF16), kv[window, 128 * h : 128 * h + 256], preferred_element_type=F32
            )
            mixed = (mixed / weight).astype(BF16)
            term = jnp.dot(mixed, wo[h], preferred_element_type=F32)
            total = term if total is None else total + term
        return total

    def half_right():
        return remote(part_out.at[0, LOW], ring_in.at[0], r_send.at[0], r_recv.at[0], dx=1)

    def half_left():
        return remote(part_out.at[0, HIGH], ring_in.at[1], r_send.at[1], r_recv.at[1], dx=-1)

    def to_right():
        return remote(part_out.at[1], part_in.at[0], r_send.at[2], r_recv.at[2], dx=1)

    def to_left():
        return remote(part_out.at[2], part_in.at[1], r_send.at[3], r_recv.at[3], dx=-1)

    def attend_step(k, carry):
        d = jnp.where(k == 0, 2, jnp.where(k == 1, 1, jnp.where(k == 2, 3, 0)))
        own_part[...] = attend(around(x, d))

        @pl.when(k == 0)
        def _():
            part_out[0] = own_part[...].astype(BF16)
            half_right().start()
            half_left().start()
            for part in (1, 0):
                hand_on(part, 1)

        @pl.when(k == 1)
        def _():
            half_right().wait_recv()
            part_out[1, LOW] = (own_part[LOW, :] + ring_in[0].astype(F32)).astype(BF16)
            part_out[1, HIGH] = own_part[HIGH, :].astype(BF16)
            to_right().start()
            for part in (1, 0):
                hand_on(part, 2)

        @pl.when(k == 2)
        def _():
            half_left().wait_recv()
            part_out[2, LOW] = own_part[LOW, :].astype(BF16)
            part_out[2, HIGH] = (own_part[HIGH, :] + ring_in[1].astype(F32)).astype(BF16)
            to_left().start()
            for part in (1, 0):
                hand_on(part, 3)

        return carry

    lax.fori_loop(0, 4, attend_step, 0)

    attended = emb[...] + own_part[...] + out_bias[...].astype(F32)
    to_right().wait_recv()
    attended = attended + part_in[0].astype(F32)
    to_left().wait_recv()
    attended = attended + part_in[1].astype(F32)
    own_part[...] = attended
    n2[c] = norm_rows(attended, ln2_gain[...], ln2_bias[...]).astype(BF16)
    give = remote(n2.at[c], n2.at[c], m_send.at[0], m_recv.at[0], dc=1)
    give.start()
    give.wait_recv()

    tokens = n2[...].reshape(2 * TOK, WIDTH)

    def hidden_of(weights, biases):
        def step(i, carry):
            at = pl.ds(pl.multiple_of(i * 384, 384), 384)
            inner = lax.dot_general(tokens, weights[at, :], NT, preferred_element_type=F32)
            hid[:, at] = gelu(inner + biases[0:1, at]).astype(BF16)
            return carry

        lax.fori_loop(0, 3, step, 0)

    def project_hidden(weights, first):
        def step(i, carry):
            at = pl.ds(pl.multiple_of(i * 384, 384), 384)
            got = jnp.dot(hid[...], weights[WIDTH : 2 * WIDTH, at], preferred_element_type=F32)
            mlp[:, at] = got if first else mlp[:, at] + got
            return carry

        lax.fori_loop(0, 3, step, 0)

    hidden_of(f_own, bias_own)
    project_hidden(f_own, True)
    for part in (0, 1):
        for k in range(4):
            for i in range(2):
                hand_copy(part, k, i).wait_recv()
    cross_v.wait_recv()
    hidden_of(f_far, bias_far)
    project_hidden(f_far, False)

    mine_at = pl.ds(pl.multiple_of(c * TOK, TOK), TOK)
    other_at = pl.ds(pl.multiple_of((1 - c) * TOK, TOK), TOK)
    mlp_out[...] = mlp[other_at, :].astype(BF16)
    back = remote(mlp_out, mlp_in, m_send.at[1], m_recv.at[1], dc=1)
    back.start()
    mine_sum = own_part[...] + fc2_bias[...].astype(F32) + mlp[mine_at, :]
    back.wait_recv()
    out[...] = (mine_sum + mlp_in[...].astype(F32)).astype(BF16)

    for copy in copies_a + copies_as + copies_n + copies_s + copies_b + copies_bs:
        copy.wait_send()
    for up, down in copies_k:
        pl.when(has_next)(up.wait_send)
        pl.when(has_prev)(down.wait_send)
    pl.when(has_next)(seg_up.wait_send)
    pl.when(has_prev)(seg_down.wait_send)
    for copy in [cross, cross_v, give, back, on_right, on_left]:
        copy.wait_send()
    for copy in [half_right(), half_left(), to_right(), to_left()]:
        copy.wait_send()
    for part in (0, 1):
        for i in range(3):
            first_copy(part, i).wait_send()
        for k in range(4):
            for i in range(2):
                second_copy(part, k, i).wait_send()
                hand_copy(part, k, i).wait_send()


def layer_call(*operands):
    vmem = pl.BlockSpec(memory_space=pltpu.VMEM)
    hbm = pl.BlockSpec(memory_space=pl.ANY)
    dma = pltpu.SemaphoreType.DMA
    scratch = [
        pltpu.VMEM((TOK, WIDTH), F32),
        pltpu.VMEM((4, TOK, WIDTH), BF16),
        pltpu.VMEM((3, 4, 8, 256), F32),
        pltpu.VMEM((4, 8, WINDOW), F32),
        pltpu.VMEM((4, TOK, 128), F32),
        pltpu.VMEM((4, QROWS, WIDTH), BF16),
        pltpu.VMEM((4, OROWS, WIDTH), BF16),
        pltpu.VMEM((WIDTH, WIDTH), BF16),
        pltpu.VMEM((4, 256, WIDTH), BF16),
        pltpu.VMEM((ROW, 512), BF16),
        pltpu.VMEM((3 * ROW, 640), BF16),
        pltpu.VMEM((3, TOK, WIDTH), BF16),
        pltpu.VMEM((2, TOK, WIDTH), BF16),
        pltpu.VMEM((TOK, WIDTH), F32),
        pltpu.VMEM((2 * WIDTH, WIDTH), BF16),
        pltpu.VMEM((2 * WIDTH, WIDTH), BF16),
        pltpu.VMEM((8, WIDTH), F32),
        pltpu.VMEM((8, WIDTH), F32),
        pltpu.VMEM((3 * HEAD, WIDTH), BF16),
        pltpu.VMEM((HEAD, WIDTH), BF16),
        pltpu.VMEM((2, 96, WIDTH), BF16),
        pltpu.VMEM((2, TOK, WIDTH), BF16),
        pltpu.VMEM((2 * TOK, WIDTH), BF16),
        pltpu.VMEM((2 * TOK, WIDTH), F32),
        pltpu.VMEM((TOK, WIDTH), BF16),
        pltpu.VMEM((TOK, WIDTH), BF16),
        dma((6,)),
    ]
    for shape in ((4,), (3,), (4,), (3,), (4,), (5,), (2, 4), (2,), (2, 3), (2, 4, 4), (4,), (2,)):
        scratch += [dma(shape), dma(shape)]
    return pl.pallas_call(
        layer_kernel,
        out_shape=jax.ShapeDtypeStruct((TOK, WIDTH), BF16),
        in_specs=[vmem] * 13 + [hbm] * 5,
        out_specs=vmem,
        scratch_shapes=scratch,
        compiler_params=pltpu.CompilerParams(
            collective_id=0, has_side_effects=True, vmem_limit_bytes=60 << 20
        ),
        name="encoder_layer",
    )(*operands)


def per_device(
    patches,
    seg_ids,
    pos_rows,
    pos_cols,
    row_table,
    col_table,
    ln1_gain,
    ln1_bias,
    w_qkv,
    w_out,
    out_bias,
    ln2_gain,
    ln2_bias,
    w_fc1,
    fc1_bias,
    w_fc2,
    fc2_bias,
):
    rest = w_fc2.shape[0] - 1024
    w_1 = w_fc1.T
    w_tail = jnp.concatenate(
        [jnp.pad(w[1024:], ((0, 128 - rest), (0, 0))) for w in (w_1, w_fc2)], axis=0
    )
    return layer_call(
        patches[0],
        seg_ids,
        pos_rows,
        pos_cols,
        row_table,
        col_table,
        ln1_gain[None],
        ln1_bias[None],
        ln2_gain[None],
        ln2_bias[None],
        out_bias[None],
        fc2_bias[None],
        jnp.pad(fc1_bias.astype(F32), (0, WIDTH - fc1_bias.shape[0]))[None],
        w_qkv.T,
        w_out,
        w_1,
        w_fc2,
        w_tail,
    )[None]


def solution(mesh):
    torus = Mesh(mesh.devices.reshape(4, 4, 4, 2, 2), AXES)
    in_specs = (
        P(BATCH, SEQ, None),
        P(BATCH, SEQ),
        P(BATCH, SEQ),
        P(BATCH, SEQ),
        P(),
        P(),
        P(),
        P(),
        P(None, SEQ),
        P(SEQ, None),
        P(),
        P(),
        P(),
        P(None, ("zh", "c")),
        P(("zh", "c")),
        P(("zh", "c"), None),
        P(),
    )
    return jax.shard_map(
        per_device,
        mesh=torus,
        in_specs=in_specs,
        out_specs=P(BATCH, SEQ, None),
        check_vma=False,
    )
```

time: 130 us -> 118 us (0.908)
  Pallas kernels: 113 us -> 104 us
  other arithmetic: 6.61 us -> 1.54 us
  local copies, waits for them, and re-layouts: 9.99 us -> 12 us
    pallas_call x1, Pallas kernels: 113 us -> 104 us  [layer_call(): pl.pallas_call(layer_kernel, out_shape=jax.ShapeDtypeStruct((TOK, WIDTH),...]
    broadcast_in_dim x1 -> x7, local copies, waits for them, and re-layouts: 0.01 us -> 8.31 us  [the longest x1 1.29 us: per_device(): ln1_gain[None]]
    concatenate x3 -> x1, other arithmetic: 6.6 us -> 0.85 us  [per_device(): jnp.concatenate([jnp.pad(w[1024:], ((0, 128 - rest), (0, 0))) for w in (w...]
    unnamed x24 -> x1, local copies, waits for them, and re-layouts: 5.95 us -> 1.81 us
    pad x2 -> x0, local copies, waits for them, and re-layouts: 1.31 us -> none  [the longest x1 0.7 us: per_device(): w_b = jnp.pad(w_out, ((8, OROWS - HEAD - 8), (0, 0)))]
where the time goes in v2:
time: 118 us
  Pallas kernels  104 us (88%)
  local copies, waits for them, and re-layouts  12 us (10%)
  other arithmetic  1.54 us (1%)
    pallas_call x1, Pallas kernels, layer_call(): pl.pallas_call(layer_kernel, out_shape=jax.ShapeDtypeStruct((TOK, WIDTH),...  104 us

profile of v2, /device:TPU:1, one launch (start us, length us, event | category | flops | bytes accessed | tf_op | source)
XLA Modules:
  0.0 117.5 jit_solution(5540402620844806840)
XLA Ops:
  0.0 1.3 %broadcast_in_dim.26.ln1_gain = f32[1,1152]{1,0:T(1,128)} reshape(f32[1152]{0:T(1024)} %param.23) | data formatting | bytes 9216 | tf_op jit(solution)/shard_map/broadcast_in_dim | solution.py:611
  1.3 1.3 %broadcast_in_dim.27.ln1_bias = f32[1,1152]{1,0:T(1,128)} reshape(f32[1152]{0:T(1024)} %param.24) | data formatting | bytes 9216 | tf_op jit(solution)/shard_map/broadcast_in_dim | solution.py:612
  2.6 1.3 %broadcast_in_dim.30.out_bias = bf16[1,1152]{1,0:T(2,128)(2,1)} reshape(bf16[1152]{0:T(1024)(128)(2,1)} %param.27) | data formatting | bytes 4608 | tf_op jit(solution)/shard_map/broadcast_in_dim | solution.py:615
  3.9 1.3 %broadcast_in_dim.28.ln2_gain = f32[1,1152]{1,0:T(1,128)} reshape(f32[1152]{0:T(1024)} %param.28) | data formatting | bytes 9216 | tf_op jit(solution)/shard_map/broadcast_in_dim | solution.py:613
  5.1 1.3 %broadcast_in_dim.29.ln2_bias = f32[1,1152]{1,0:T(1,128)} reshape(f32[1152]{0:T(1024)} %param.29) | data formatting | bytes 9216 | tf_op jit(solution)/shard_map/broadcast_in_dim | solution.py:614
  6.4 1.3 %broadcast_in_dim.31.fc2_bias = bf16[1,1152]{1,0:T(2,128)(2,1)} reshape(bf16[1152]{0:T(1024)(128)(2,1)} %param.33) | data formatting | bytes 4608 | tf_op jit(solution)/shard_map/broadcast_in_dim | solution.py:616
  7.7 0.7 pad_convert_fusion
  8.4 0.6 reshape.fc1_bias
  9.0 0.9 slice.8
  9.9 0.9 slice.7
  10.8 0.9 fusion.2.w_tail
  11.7 104.0 %encoder_layer.1 = bf16[192,1152]{1,0:T(8,128)(2,1)} custom-call(bf16[192,1152]{1,0:T(8,128)(2,1)} %bitcast.8, s32[1,192]{1,0:T(1,128)} %seg_in.1, s32[1,192]{1,0:T(1,128)} %rows_in.1, s32[1,192]{1,0:T(1,128)} %cols_in.1, bf16[64,1152]{1,0:T(8,128)(2,1)} %rows_tab.1, bf16[64,1152]{1,0:T(8,128)(2,1)} %cols_tab.1, f32[1,1152]{1,0:T(1,128)} %broadcast_in_dim.26.ln1_gain, ...), custom_call_target="tpu_custom_call" | custom-call | tf_op jit(solution)/shard_map/encoder_layer/pallas_call | solution.py:567
  115.7 1.8 %copy.19 = bf16[1,192,1152]{2,1,0:T(8,128)(2,1)} copy(bf16[1,192,1152]{2,1,0:T(8,128)(2,1)} %bitcast.6) | data formatting | bytes 884736

commit v3 on v2

--- a/solution.py
+++ b/solution.py
@@ -16,9 +16,7 @@
 WIDTH = 1152
 ROW = 4 * TOK
 HEAD = 72
-WINDOW = 9 * TOK
 QROWS = 224
-OROWS = 96
 F32 = jnp.float32
 BF16 = jnp.bfloat16
 NT = (((1,), (1,)), ((), ()))
@@ -29,6 +27,10 @@
     moved = values - center
     spread = jnp.mean(jnp.square(moved), -1, keepdims=True)
     return moved * lax.rsqrt(spread + 1e-06) * gain + shift
+
+
+def line(ref):
+    return ref[...].astype(F32).reshape(1, WIDTH)
 
 
 def gelu(u):
@@ -53,7 +55,8 @@
     w_b,
     w_1,
     w_2,
-    w_tail,
+    tail_1,
+    tail_2,
     out,
     emb,
     nrm,
@@ -61,13 +64,16 @@
     seg_keys,
     seg_query,
     wz,
-    wb,
     wp,
-    wo,
+    wof,
+    pick,
+    mixed_out,
+    mixed_in,
+    top_own,
+    sum_own,
+    mix_own,
     qs,
     kv,
-    part_out,
-    part_in,
     own_part,
     f_own,
     f_far,
@@ -75,7 +81,6 @@
     bias_far,
     stage_a,
     stage_b,
-    ring_in,
     n2,
     hid,
     mlp,
@@ -102,6 +107,8 @@
     f1_recv,
     f2_send,
     f2_recv,
+    bx_send,
+    bx_recv,
     r_send,
     r_recv,
     m_send,
@@ -151,24 +158,9 @@
         pltpu.make_async_copy(w_b, stage_b, loc_sem.at[1]),
         pltpu.make_async_copy(w_1.at[0:1024], f_own.at[0:1024], loc_sem.at[2]),
         pltpu.make_async_copy(w_2.at[0:1024], f_own.at[1152:2176], loc_sem.at[3]),
-        pltpu.make_async_copy(w_tail.at[0:128], f_own.at[1024:1152], loc_sem.at[4]),
-        pltpu.make_async_copy(w_tail.at[128:256], f_own.at[2176:2304], loc_sem.at[5]),
     ]
     for copy in local:
         copy.start()
-
-    def wide(ref):
-        return jnp.concatenate([ref[...].astype(F32), jnp.zeros((1, 64), F32)], axis=1)
-
-    level = lax.broadcasted_iota(jnp.int32, (128, 256), 0).astype(F32)
-    wanted = jnp.where(level < 64.0, wide(rows_in), wide(cols_in) + 64.0)
-    hot = jnp.transpose(jnp.where(level == wanted, 1.0, 0.0))[:TOK].astype(BF16)
-    tables = jnp.concatenate([rows_tab[...], cols_tab[...]], axis=0)
-    embedded = patches[...].astype(F32) + jnp.dot(hot, tables, preferred_element_type=F32)
-    emb[...] = embedded
-    nrm[x] = norm_rows(embedded, ln1_gain[...], ln1_bias[...]).astype(BF16)
-    segs[1, x] = jnp.broadcast_to(wide(seg_in), (8, 256))
-    bias_own[...] = jnp.broadcast_to(fc1_bias[...], (8, WIDTH))
 
     local[0].wait()
     staged = stage_a[...].astype(F32)
@@ -190,6 +182,19 @@
     ]
     for copy in copies_a:
         copy.start()
+
+    def wide(ref):
+        return jnp.concatenate([ref[...].astype(F32), jnp.zeros((1, 64), F32)], axis=1)
+
+    level = lax.broadcasted_iota(jnp.int32, (128, 256), 0).astype(F32)
+    wanted = jnp.where(level < 64.0, wide(rows_in), wide(cols_in) + 64.0)
+    hot = jnp.transpose(jnp.where(level == wanted, 1.0, 0.0))[:TOK].astype(BF16)
+    tables = jnp.concatenate([rows_tab[...], cols_tab[...]], axis=0)
+    embedded = patches[...].astype(F32) + jnp.dot(hot, tables, preferred_element_type=F32)
+    emb[...] = embedded
+    nrm[x] = norm_rows(embedded, line(ln1_gain), line(ln1_bias)).astype(BF16)
+    segs[1, x] = jnp.broadcast_to(wide(seg_in), (8, 256))
+    bias_own[...] = jnp.broadcast_to(line(fc1_bias), (8, WIDTH))
 
     LOW, HIGH = pl.ds(0, 96), pl.ds(96, 96)
     copies_n = [
@@ -207,26 +212,18 @@
         at = pl.multiple_of((py * 4 + px) * 144 + first, 16)
         return f_far.at[pl.ds(at, rows)]
 
-    for copy in local[2:]:
-        copy.wait()
-    mine = pl.ds(pl.multiple_of((y * 4 + x) * 144, 16), 144)
-    cross = remote(f_own.at[mine], f_far.at[mine], f_send.at[0], f_recv.at[0], mirror=True)
-    cross_v = remote(bias_own, bias_far, f_send.at[1], f_recv.at[1], mirror=True)
-    cross.start()
-    cross_v.start()
-
     local[1].wait()
-    wb[zl] = jnp.concatenate(
-        [
-            jnp.zeros((8, WIDTH), F32),
-            stage_b[...].astype(F32),
-            jnp.zeros((OROWS - HEAD - 8, WIDTH), F32),
-        ],
-        axis=0,
+    wof[x, pl.ds(pl.multiple_of(zl * 80, 16), 80)] = jnp.concatenate(
+        [stage_b[...].astype(F32), jnp.zeros((8, WIDTH), F32)], axis=0
     ).astype(BF16)
 
     wp[...] = jnp.zeros_like(wp)
-    wo[...] = jnp.zeros_like(wo)
+    lane = lax.broadcasted_iota(jnp.int32, (256, 384), 1)
+    line_of = lax.broadcasted_iota(jnp.int32, (256, 384), 0)
+    for h in range(4):
+        feature = lane - 80 * h
+        chosen = (line_of - (16 * h + HEAD) == feature) & (feature >= 0) & (feature < HEAD)
+        pick[h] = jnp.where(chosen, 1.0, 0.0).astype(BF16)
 
     @pl.when(jnp.logical_not(has_prev))
     def _():
@@ -235,7 +232,7 @@
 
     @pl.when(jnp.logical_not(has_next))
     def _():
-        kv[2 * ROW : 3 * ROW, :] = jnp.zeros((ROW, 640), BF16)
+        kv[ROW : 2 * ROW, :] = jnp.zeros((ROW, 640), BF16)
         segs[2] = jnp.full((4, 8, 256), -1.0, F32)
 
     left, right, far_x = around(x, -1), around(x, 1), around(x, 2)
@@ -270,8 +267,8 @@
     def project(k, source):
         tokens = nrm[source]
         at = pl.ds(pl.multiple_of(source * TOK, TOK), TOK)
-        here = pl.ds(pl.multiple_of(ROW + source * TOK, TOK), TOK)
-        as_next = pl.ds(pl.multiple_of(2 * ROW + source * TOK, TOK), TOK)
+        here = pl.ds(pl.multiple_of(2 * ROW + source * TOK, TOK), TOK)
+        as_next = pl.ds(pl.multiple_of(ROW + source * TOK, TOK), TOK)
         kv[here, :] = lax.dot_general(
             tokens, wp[512:1152, :], NT, preferred_element_type=F32
         ).astype(BF16)
@@ -284,11 +281,23 @@
             tokens, wp[0:512, :], NT, preferred_element_type=F32
         ).astype(BF16)
 
+    for copy in local[2:]:
+        copy.wait()
+    rest = w_1.shape[0] - 1024
+    mine = pl.ds(pl.multiple_of((y * 4 + x) * 144, 16), 144)
+    cross = remote(f_own.at[mine], f_far.at[mine], f_send.at[0], f_recv.at[0], mirror=True)
+    cross_v = remote(bias_own, bias_far, f_send.at[1], f_recv.at[1], mirror=True)
+    real = lax.broadcasted_iota(jnp.int32, (128, WIDTH), 0) < rest
+    f_own[1024:1152, :] = jnp.where(real, tail_1[...], jnp.zeros((128, WIDTH), BF16))
+    f_own[2176:2304, :] = jnp.where(real, tail_2[...], jnp.zeros((128, WIDTH), BF16))
+    cross.start()
+    cross_v.start()
+
     project(0, x)
     project(1, left)
     project(2, right)
 
-    PARTS = ((0, 80, 48), (80, 64, 32))
+    PARTS = ((0, 96, 48), (96, 48, 32))
     def held(part, k, db=0):
         d = (0, -1, 1, 2)[k]
         if part == 0:
@@ -331,11 +340,6 @@
         for i in range(2):
             second_copy(part, k, i).wait_recv()
             hand_copy(part, k, i).start()
-
-    cross.wait_recv()
-    for part in (0, 1):
-        start_first(part)
-        start_second(part, 0)
 
     on_right.wait_recv()
     on_left.wait_recv()
@@ -347,125 +351,178 @@
     pl.when(has_next)(seg_up.start)
     pl.when(has_prev)(seg_down.start)
 
-    half_b = c * (OROWS // 2)
-    copies_b = [
-        slab(wb, half_b, 48, b_send, b_recv, 0, 1),
-        slab(wb, half_b, 48, b_send, b_recv, 1, -1),
-        slab(wb, half_b, 32, b_send, b_recv, 2, 2),
-        slab(wb, half_b + 32, 16, b_send, b_recv, 3, -2),
-    ]
-    for copy in copies_b:
-        copy.start()
-
+    B_CUTS = ((0, 48), (48, 32))
+
+    def rows_of(owner, core):
+        first, rows = B_CUTS[core]
+        return pl.ds(pl.multiple_of(owner * 80 + first, 16), rows)
+
+    def b_copies(core):
+        ref = wof.at[x, rows_of(zl, core)]
+        return [
+            remote(ref, ref, b_send.at[k], b_recv.at[k], dz=dz)
+            for k, dz in enumerate((1, -1, (2, -2)[core]))
+        ]
+
+    def bs_copies(core):
+        made = []
+        for k, d in enumerate((-1, 1, 2)):
+            ref = wof.at[x, rows_of(around(zl, d), core)]
+            made.append(remote(ref, ref, bs_send.at[k], bs_recv.at[k], dc=1))
+        return made
+
+    def each_core(act):
+        for core in (0, 1):
+
+            @pl.when(c == core)
+            def _():
+                act(core)
+
+    def start_b(core):
+        for copy in b_copies(core):
+            copy.start()
+
+    def pass_b(core):
+        for copy in b_copies(core):
+            copy.wait_recv()
+        for copy in bs_copies(core):
+            copy.start()
+
+    def take_b(core):
+        for copy in bs_copies(1 - core):
+            copy.wait_recv()
+
+    def end_b(core):
+        for copy in b_copies(core) + bs_copies(core):
+            copy.wait_send()
+
+    half_o = pl.ds(pl.multiple_of(c * 160, 16), 160)
+
+    def bx_copy(k):
+        ref = wof.at[x, half_o]
+        return remote(ref, ref, bx_send.at[k], bx_recv.at[k], dx=(1, -1, 2)[k])
+
+    def bxs_copy(k):
+        ref = wof.at[around(x, (-1, 1, 2)[k]), half_o]
+        return remote(ref, ref, bx_send.at[3 + k], bx_recv.at[3 + k], dc=1)
+
+    each_core(start_b)
+
+    cross.wait_recv()
+    for part in (0, 1):
+        start_first(part)
+        start_second(part, 0)
+
+    scale = 1.0 / math.sqrt(HEAD)
+    seg_keys[0] = jnp.concatenate([segs[1, b][:, :TOK] for b in range(4)] + [segs[1, 0][:, :TOK]], axis=1)
+    for j in range(4):
+        spread = jnp.concatenate([segs[1, j]] * 16, axis=0)
+        seg_query[j] = jnp.transpose(spread)[:TOK]
+
+    def scores_of(j, h, keys):
+        at = pl.ds(pl.multiple_of(j * TOK, TOK), TOK)
+        return lax.dot_general(
+            qs[at, 128 * h : 128 * h + 128],
+            kv[keys, 128 * h : 128 * h + 128],
+            NT,
+            preferred_element_type=F32,
+        )
+
+    def attend_own(j):
+        same = seg_query[j][:, 0:1] == seg_keys[0][0:1, :ROW]
+        own = pl.ds(2 * ROW, ROW)
+        for h in range(4):
+            scores = jnp.where(same, scores_of(j, h, own), -jnp.inf)
+            top = jnp.max(scores, -1, keepdims=True)
+            expo = jnp.exp((scores - top) * scale)
+            top_own[j, h] = jnp.broadcast_to(top, (TOK, 128))
+            sum_own[j, h] = jnp.broadcast_to(jnp.sum(expo, -1, keepdims=True), (TOK, 128))
+            mix_own[j, h] = jnp.dot(
+                expo.astype(BF16), kv[own, 128 * h : 128 * h + 256], preferred_element_type=F32
+            )
+
+    def own_steps(first):
+        def step(j, carry):
+            attend_own(j)
+            return carry
+
+        lax.fori_loop(first, first + 2, step, 0)
+
+    own_steps(0)
     for k in (1, 2, 3):
         for part in (1, 0):
             first_copy(part, k - 1).wait_recv()
             start_second(part, k)
+    each_core(pass_b)
+    each_core(take_b)
+    for k in range(3):
+        bx_copy(k).start()
+    own_steps(2)
     for part in (1, 0):
         hand_on(part, 0)
 
-    copies_bs = to_sibling(wb, half_b, OROWS // 2, bs_send, bs_recv)
-    for copy in copies_b:
-        copy.wait_recv()
-    for copy in copies_bs:
-        copy.start()
-
     pl.when(has_prev)(seg_up.wait_recv)
     pl.when(has_next)(seg_down.wait_recv)
+    around_segs = [segs[r, b][:, :TOK] for r in (0, 2) for b in range(4)]
     for j in range(4):
-        parts = [segs[b // 4, b % 4][:, :TOK] for b in range(j, j + 9)]
-        seg_keys[j] = jnp.concatenate(parts, axis=1)
-        mine_seg = segs[1, j]
-        spread = jnp.concatenate([mine_seg] * 16, axis=0)
-        seg_query[j] = jnp.transpose(spread)[:TOK]
-    for copy in copies_bs:
-        copy.wait_recv()
-    for h in range(4):
-        wo[h, 16 * h + 64 : 16 * h + 64 + OROWS, :] = wb[h]
-
+        seg_keys[j] = jnp.concatenate(around_segs[j : j + 5], axis=1)
     for up, down in copies_k:
         pl.when(has_prev)(up.wait_recv)
         pl.when(has_next)(down.wait_recv)
 
-    scale = 1.0 / math.sqrt(HEAD)
-
     def attend(j):
-        at = pl.ds(pl.multiple_of(j * TOK, TOK), TOK)
-        window = pl.ds(pl.multiple_of(j * TOK, TOK), WINDOW)
+        window = pl.ds(pl.multiple_of(j * TOK, TOK), 5 * TOK)
         same = seg_query[j][:, 0:1] == seg_keys[j][0:1, :]
         total = None
         for h in range(4):
-            scores = lax.dot_general(
-                qs[at, 128 * h : 128 * h + 128],
-                kv[window, 128 * h : 128 * h + 128],
-                NT,
-                preferred_element_type=F32,
-            )
-            scores = jnp.where(same, scores, -jnp.inf)
-            top = jnp.max(scores, -1, keepdims=True)
+            scores = jnp.where(same, scores_of(j, h, window), -jnp.inf)
+            before = top_own[j, h][:, 0:1]
+            top = jnp.maximum(jnp.max(scores, -1, keepdims=True), before)
             expo = jnp.exp((scores - top) * scale)
-            weight = jnp.sum(expo, -1, keepdims=True)
+            kept = jnp.exp((before - top) * scale)
+            weight = jnp.sum(expo, -1, keepdims=True) + kept * sum_own[j, h][:, 0:1]
             mixed = jnp.dot(
                 expo.astype(BF16), kv[window, 128 * h : 128 * h + 256], preferred_element_type=F32
             )
-            mixed = (mixed / weight).astype(BF16)
-            term = jnp.dot(mixed, wo[h], preferred_element_type=F32)
+            mixed = ((mixed + kept * mix_own[j, h]) / weight).astype(BF16)
+            term = jnp.dot(mixed, pick[h], preferred_element_type=F32)
             total = term if total is None else total + term
-        return total
-
-    def half_right():
-        return remote(part_out.at[0, LOW], ring_in.at[0], r_send.at[0], r_recv.at[0], dx=1)
-
-    def half_left():
-        return remote(part_out.at[0, HIGH], ring_in.at[1], r_send.at[1], r_recv.at[1], dx=-1)
-
-    def to_right():
-        return remote(part_out.at[1], part_in.at[0], r_send.at[2], r_recv.at[2], dx=1)
-
-    def to_left():
-        return remote(part_out.at[2], part_in.at[1], r_send.at[3], r_recv.at[3], dx=-1)
+        return total.astype(BF16)
+
+    def mixed_copy(k):
+        return remote(
+            mixed_out.at[k], mixed_in.at[k], r_send.at[k], r_recv.at[k], dx=(2, 1, -1)[k]
+        )
 
     def attend_step(k, carry):
         d = jnp.where(k == 0, 2, jnp.where(k == 1, 1, jnp.where(k == 2, 3, 0)))
-        own_part[...] = attend(around(x, d))
-
-        @pl.when(k == 0)
-        def _():
-            part_out[0] = own_part[...].astype(BF16)
-            half_right().start()
-            half_left().start()
-            for part in (1, 0):
-                hand_on(part, 1)
-
-        @pl.when(k == 1)
-        def _():
-            half_right().wait_recv()
-            part_out[1, LOW] = (own_part[LOW, :] + ring_in[0].astype(F32)).astype(BF16)
-            part_out[1, HIGH] = own_part[HIGH, :].astype(BF16)
-            to_right().start()
-            for part in (1, 0):
-                hand_on(part, 2)
-
-        @pl.when(k == 2)
-        def _():
-            half_left().wait_recv()
-            part_out[2, LOW] = own_part[LOW, :].astype(BF16)
-            part_out[2, HIGH] = (own_part[HIGH, :] + ring_in[1].astype(F32)).astype(BF16)
-            to_left().start()
-            for part in (1, 0):
-                hand_on(part, 3)
+        got = attend(around(x, d))
+        mixed_out[k] = got
+        for step in range(3):
+
+            @pl.when(k == step)
+            def _():
+                mixed_copy(step).start()
+                for part in (1, 0):
+                    hand_on(part, step + 1)
+                bx_copy(step).wait_recv()
+                bxs_copy(step).start()
 
         return carry
 
     lax.fori_loop(0, 4, attend_step, 0)
 
-    attended = emb[...] + own_part[...] + out_bias[...].astype(F32)
-    to_right().wait_recv()
-    attended = attended + part_in[0].astype(F32)
-    to_left().wait_recv()
-    attended = attended + part_in[1].astype(F32)
+    def projected(held_in, px):
+        return jnp.dot(held_in[:, 0:320], wof[px], preferred_element_type=F32)
+
+    attended = emb[...] + projected(mixed_out[3], x) + line(out_bias)
+    for k in range(3):
+        bxs_copy(k).wait_recv()
+    for k, d in enumerate((2, -1, 1)):
+        mixed_copy(k).wait_recv()
+        attended = attended + projected(mixed_in[k], around(x, d))
     own_part[...] = attended
-    n2[c] = norm_rows(attended, ln2_gain[...], ln2_bias[...]).astype(BF16)
+    n2[c] = norm_rows(attended, line(ln2_gain), line(ln2_bias)).astype(BF16)
     give = remote(n2.at[c], n2.at[c], m_send.at[0], m_recv.at[0], dc=1)
     give.start()
     give.wait_recv()
@@ -505,11 +562,11 @@
     mlp_out[...] = mlp[other_at, :].astype(BF16)
     back = remote(mlp_out, mlp_in, m_send.at[1], m_recv.at[1], dc=1)
     back.start()
-    mine_sum = own_part[...] + fc2_bias[...].astype(F32) + mlp[mine_at, :]
+    mine_sum = own_part[...] + line(fc2_bias) + mlp[mine_at, :]
     back.wait_recv()
     out[...] = (mine_sum + mlp_in[...].astype(F32)).astype(BF16)
 
-    for copy in copies_a + copies_as + copies_n + copies_s + copies_b + copies_bs:
+    for copy in copies_a + copies_as + copies_n + copies_s:
         copy.wait_send()
     for up, down in copies_k:
         pl.when(has_next)(up.wait_send)
@@ -518,8 +575,11 @@
     pl.when(has_prev)(seg_down.wait_send)
     for copy in [cross, cross_v, give, back, on_right, on_left]:
         copy.wait_send()
-    for copy in [half_right(), half_left(), to_right(), to_left()]:
-        copy.wait_send()
+    each_core(end_b)
+    for k in range(3):
+        bx_copy(k).wait_send()
+        bxs_copy(k).wait_send()
+        mixed_copy(k).wait_send()
     for part in (0, 1):
         for i in range(3):
             first_copy(part, i).wait_send()
@@ -532,21 +592,25 @@
 def layer_call(*operands):
     vmem = pl.BlockSpec(memory_space=pltpu.VMEM)
     hbm = pl.BlockSpec(memory_space=pl.ANY)
+    edge = pl.BlockSpec((128, WIDTH), lambda i: (8, 0))
     dma = pltpu.SemaphoreType.DMA
     scratch = [
         pltpu.VMEM((TOK, WIDTH), F32),
         pltpu.VMEM((4, TOK, WIDTH), BF16),
         pltpu.VMEM((3, 4, 8, 256), F32),
-        pltpu.VMEM((4, 8, WINDOW), F32),
+        pltpu.VMEM((4, 8, 5 * TOK), F32),
         pltpu.VMEM((4, TOK, 128), F32),
         pltpu.VMEM((4, QROWS, WIDTH), BF16),
-        pltpu.VMEM((4, OROWS, WIDTH), BF16),
         pltpu.VMEM((WIDTH, WIDTH), BF16),
-        pltpu.VMEM((4, 256, WIDTH), BF16),
+        pltpu.VMEM((4, 320, WIDTH), BF16),
+        pltpu.VMEM((4, 256, 384), BF16),
+        pltpu.VMEM((4, TOK, 384), BF16),
+        pltpu.VMEM((3, TOK, 384), BF16),
+        pltpu.VMEM((4, 4, TOK, 128), F32),
+        pltpu.VMEM((4, 4, TOK, 128), F32),
+        pltpu.VMEM((4, 4, TOK, 256), F32),
         pltpu.VMEM((ROW, 512), BF16),
         pltpu.VMEM((3 * ROW, 640), BF16),
-        pltpu.VMEM((3, TOK, WIDTH), BF16),
-        pltpu.VMEM((2, TOK, WIDTH), BF16),
         pltpu.VMEM((TOK, WIDTH), F32),
         pltpu.VMEM((2 * WIDTH, WIDTH), BF16),
         pltpu.VMEM((2 * WIDTH, WIDTH), BF16),
@@ -554,20 +618,20 @@
         pltpu.VMEM((8, WIDTH), F32),
         pltpu.VMEM((3 * HEAD, WIDTH), BF16),
         pltpu.VMEM((HEAD, WIDTH), BF16),
-        pltpu.VMEM((2, 96, WIDTH), BF16),
         pltpu.VMEM((2, TOK, WIDTH), BF16),
         pltpu.VMEM((2 * TOK, WIDTH), BF16),
         pltpu.VMEM((2 * TOK, WIDTH), F32),
         pltpu.VMEM((TOK, WIDTH), BF16),
         pltpu.VMEM((TOK, WIDTH), BF16),
-        dma((6,)),
+        dma((4,)),
     ]
-    for shape in ((4,), (3,), (4,), (3,), (4,), (5,), (2, 4), (2,), (2, 3), (2, 4, 4), (4,), (2,)):
+    for shape in ((4,), (3,), (4,), (3,), (4,), (5,), (2, 4), (2,), (2, 3), (2, 4, 4), (6,), (3,), (2,)):
         scratch += [dma(shape), dma(shape)]
     return pl.pallas_call(
         layer_kernel,
         out_shape=jax.ShapeDtypeStruct((TOK, WIDTH), BF16),
-        in_specs=[vmem] * 13 + [hbm] * 5,
+        grid=(1,),
+        in_specs=[vmem] * 13 + [hbm] * 4 + [edge] * 2,
         out_specs=vmem,
         scratch_shapes=scratch,
         compiler_params=pltpu.CompilerParams(
@@ -596,11 +660,7 @@
     w_fc2,
     fc2_bias,
 ):
-    rest = w_fc2.shape[0] - 1024
     w_1 = w_fc1.T
-    w_tail = jnp.concatenate(
-        [jnp.pad(w[1024:], ((0, 128 - rest), (0, 0))) for w in (w_1, w_fc2)], axis=0
-    )
     return layer_call(
         patches[0],
         seg_ids,
@@ -608,18 +668,19 @@
         pos_cols,
         row_table,
         col_table,
-        ln1_gain[None],
-        ln1_bias[None],
-        ln2_gain[None],
-        ln2_bias[None],
-        out_bias[None],
-        fc2_bias[None],
-        jnp.pad(fc1_bias.astype(F32), (0, WIDTH - fc1_bias.shape[0]))[None],
+        ln1_gain,
+        ln1_bias,
+        ln2_gain,
+        ln2_bias,
+        out_bias,
+        fc2_bias,
+        jnp.pad(fc1_bias, (0, WIDTH - fc1_bias.shape[0])),
         w_qkv.T,
         w_out,
         w_1,
         w_fc2,
-        w_tail,
+        w_1,
+        w_fc2,
     )[None]
 
 

time: 118 us -> 111 us (0.941)
  local copies, waits for them, and re-layouts: 12 us -> 3.09 us
  Pallas kernels: 104 us -> 107 us
  other arithmetic: 1.54 us -> 0 us
    broadcast_in_dim x7 -> x0, local copies, waits for them, and re-layouts: 8.31 us -> none  [the longest x1 1.29 us: per_device(): ln1_gain[None]]
    pallas_call x1, Pallas kernels: 104 us -> 107 us  [layer_call(): pl.pallas_call(layer_kernel, out_shape=jax.ShapeDtypeStruct((TOK, WIDTH),...]
    slice x2 -> x0, local copies, waits for them, and re-layouts: 1.83 us -> none  [per_device(): w[1024:]]
    pad x0 -> x1, local copies, waits for them, and re-layouts: none -> 1.28 us  [per_device(): jnp.pad(fc1_bias, (0, WIDTH - fc1_bias.shape[0]))]
where the time goes in v3:
time: 111 us; the launch traced here: 110 us
  Pallas kernels  107 us (96%)
  local copies, waits for them, and re-layouts  3.09 us (3%)
    pallas_call x1, Pallas kernels, layer_call(): pl.pallas_call(layer_kernel, out_shape=jax.ShapeDtypeStruct((TOK, WIDTH),...  107 us

profile of v3, /device:TPU:1, one launch (start us, length us, event | category | flops | bytes accessed | tf_op | source)
XLA Modules:
  0.0 110.3 jit_solution(11654477158563482946)
XLA Ops:
  0.0 1.3 %pad.4.fc1_bias = bf16[1152]{0:T(1024)(128)(2,1)} pad(bf16[1076]{0:T(1024)(128)(2,1)} %param.31, bf16[]{:T(256)} %constant.2.clone.1), padding=0_76 | pad | bytes 4458 | tf_op jit(solution)/shard_map/jit(_pad)/pad | solution.py:677
  1.3 107.2 %encoder_layer.1 = bf16[192,1152]{1,0:T(8,128)(2,1)} custom-call(bf16[192,1152]{1,0:T(8,128)(2,1)} %bitcast.8, s32[1,192]{1,0:T(1,128)} %seg_in.1, s32[1,192]{1,0:T(1,128)} %rows_in.1, s32[1,192]{1,0:T(1,128)} %cols_in.1, bf16[64,1152]{1,0:T(8,128)(2,1)} %rows_tab.1, bf16[64,1152]{1,0:T(8,128)(2,1)} %cols_tab.1, f32[1152]{0:T(1024)} %ln1_gain.1, ...), custom_call_target="tpu_custom_call" | custom-call | tf_op jit(solution)/shard_map/encoder_layer/pallas_call | solution.py:630
  108.5 1.8 %copy.19 = bf16[1,192,1152]{2,1,0:T(8,128)(2,1)} copy(bf16[1,192,1152]{2,1,0:T(8,128)(2,1)} %bitcast.6) | data formatting | bytes 884736

commit v4 on v3

--- a/solution.py
+++ b/solution.py
@@ -16,7 +16,7 @@
 WIDTH = 1152
 ROW = 4 * TOK
 HEAD = 72
-QROWS = 224
+QROWS = 256
 F32 = jnp.float32
 BF16 = jnp.bfloat16
 NT = (((1,), (1,)), ((), ()))
@@ -89,6 +89,8 @@
     loc_sem,
     a_send,
     a_recv,
+    ay_send,
+    ay_recv,
     as_send,
     as_recv,
     b_send,
@@ -165,7 +167,13 @@
     local[0].wait()
     staged = stage_a[...].astype(F32)
     wz[zl] = jnp.concatenate(
-        [staged[:HEAD], jnp.zeros((8, WIDTH), F32), staged[HEAD:]], axis=0
+        [
+            staged[:HEAD],
+            jnp.zeros((8, WIDTH), F32),
+            staged[HEAD:],
+            jnp.zeros((QROWS - 8 - 3 * HEAD, WIDTH), F32),
+        ],
+        axis=0,
     ).astype(BF16)
     pl.semaphore_wait(barrier, len(peers))
 
@@ -173,12 +181,12 @@
         ref = buf.at[zl, pl.ds(pl.multiple_of(first, 16), rows)]
         return remote(ref, ref, send.at[k], recv.at[k], dz=dz)
 
-    half_a = c * (QROWS // 2)
+    eighth = (c * 4 + y) * 32
     copies_a = [
-        slab(wz, half_a, 112, a_send, a_recv, 0, 1),
-        slab(wz, half_a, 112, a_send, a_recv, 1, -1),
-        slab(wz, half_a, 64, a_send, a_recv, 2, 2),
-        slab(wz, half_a + 64, 48, a_send, a_recv, 3, -2),
+        slab(wz, eighth, 32, a_send, a_recv, 0, 1),
+        slab(wz, eighth, 32, a_send, a_recv, 1, -1),
+        slab(wz, eighth, 16, a_send, a_recv, 2, 2),
+        slab(wz, eighth + 16, 16, a_send, a_recv, 3, -2),
     ]
     for copy in copies_a:
         copy.start()
@@ -194,7 +202,11 @@
     emb[...] = embedded
     nrm[x] = norm_rows(embedded, line(ln1_gain), line(ln1_bias)).astype(BF16)
     segs[1, x] = jnp.broadcast_to(wide(seg_in), (8, 256))
-    bias_own[...] = jnp.broadcast_to(line(fc1_bias), (8, WIDTH))
+    short = fc1_bias.shape[0]
+    wide_bias = jnp.concatenate(
+        [fc1_bias[...].astype(F32).reshape(1, short), jnp.zeros((1, WIDTH - short), F32)], axis=1
+    )
+    bias_own[...] = jnp.broadcast_to(wide_bias, (8, WIDTH))
 
     LOW, HIGH = pl.ds(0, 96), pl.ds(96, 96)
     copies_n = [
@@ -208,14 +220,93 @@
     for copy in copies_n + copies_s:
         copy.start()
 
-    def unit(py, px, first, rows):
-        at = pl.multiple_of((py * 4 + px) * 144 + first, 16)
-        return f_far.at[pl.ds(at, rows)]
-
     local[1].wait()
     wof[x, pl.ds(pl.multiple_of(zl * 80, 16), 80)] = jnp.concatenate(
         [stage_b[...].astype(F32), jnp.zeros((8, WIDTH), F32)], axis=0
     ).astype(BF16)
+
+    for copy in copies_a:
+        copy.wait_recv()
+    copies_ay = []
+    for k, d in enumerate((-1, 1, 2)):
+        for i, dy in enumerate((1, -1, 2)):
+            ref = wz.at[around(zl, d), pl.ds(pl.multiple_of(eighth, 16), 32)]
+            copies_ay.append(remote(ref, ref, ay_send.at[k, i], ay_recv.at[k, i], dy=dy))
+    for copy in copies_ay:
+        copy.start()
+
+    def unit(py, px, first, rows):
+        at = pl.multiple_of((py * 4 + px) * 144 + first, 16)
+        return f_far.at[pl.ds(at, rows)]
+
+    for copy in local[2:]:
+        copy.wait()
+    rest = w_1.shape[0] - 1024
+    mine = pl.ds(pl.multiple_of((y * 4 + x) * 144, 16), 144)
+    cross = remote(f_own.at[mine], f_far.at[mine], f_send.at[0], f_recv.at[0], mirror=True)
+    cross_v = remote(bias_own, bias_far, f_send.at[1], f_recv.at[1], mirror=True)
+    real = lax.broadcasted_iota(jnp.int32, (128, WIDTH), 0) < rest
+    f_own[1024:1152, :] = jnp.where(real, tail_1[...], jnp.zeros((128, WIDTH), BF16))
+    f_own[2176:2304, :] = jnp.where(real, tail_2[...], jnp.zeros((128, WIDTH), BF16))
+    cross.start()
+    cross_v.start()
+
+    B_CUTS = ((0, 48), (48, 32))
+
+    def rows_of(owner, core):
+        first, rows = B_CUTS[core]
+        return pl.ds(pl.multiple_of(owner * 80 + first, 16), rows)
+
+    def b_copies(core):
+        ref = wof.at[x, rows_of(zl, core)]
+        return [
+            remote(ref, ref, b_send.at[k], b_recv.at[k], dz=dz)
+            for k, dz in enumerate((1, -1, (2, -2)[core]))
+        ]
+
+    def bs_copies(core):
+        made = []
+        for k, d in enumerate((-1, 1, 2)):
+            ref = wof.at[x, rows_of(around(zl, d), core)]
+            made.append(remote(ref, ref, bs_send.at[k], bs_recv.at[k], dc=1))
+        return made
+
+    def each_core(act):
+        for core in (0, 1):
+
+            @pl.when(c == core)
+            def _():
+                act(core)
+
+    def start_b(core):
+        for copy in b_copies(core):
+            copy.start()
+
+    def pass_b(core):
+        for copy in b_copies(core):
+            copy.wait_recv()
+        for copy in bs_copies(core):
+            copy.start()
+
+    def take_b(core):
+        for copy in bs_copies(1 - core):
+            copy.wait_recv()
+
+    def end_b(core):
+        for copy in b_copies(core) + bs_copies(core):
+            copy.wait_send()
+
+    half_o = pl.ds(pl.multiple_of(c * 160, 16), 160)
+
+    def bx_copy(k):
+        ref = wof.at[x, half_o]
+        return remote(ref, ref, bx_send.at[k], bx_recv.at[k], dx=(1, -1, 2)[k])
+
+    def bxs_copy(k):
+        ref = wof.at[around(x, (-1, 1, 2)[k]), half_o]
+        return remote(ref, ref, bx_send.at[3 + k], bx_recv.at[3 + k], dc=1)
+
+    each_core(start_b)
 
     wp[...] = jnp.zeros_like(wp)
     lane = lax.broadcasted_iota(jnp.int32, (256, 384), 1)
@@ -251,8 +342,8 @@
             made.append(remote(ref, ref, send.at[k], recv.at[k], dc=1))
         return made
 
-    copies_as = to_sibling(wz, half_a, QROWS // 2, as_send, as_recv)
-    for copy in copies_a:
+    copies_as = to_sibling(wz, c * (QROWS // 2), QROWS // 2, as_send, as_recv)
+    for copy in copies_ay:
         copy.wait_recv()
     for copy in copies_as:
         copy.start()
@@ -260,7 +351,7 @@
         copy.wait_recv()
     for h in range(4):
         wp[144 * h : 144 * h + 80, :] = wz[h, 0:80, :]
-        wp[512 + 144 * h : 656 + 144 * h, :] = wz[h, 80:QROWS, :]
+        wp[512 + 144 * h : 656 + 144 * h, :] = wz[h, 80:224, :]
 
     copies_k = []
 
@@ -281,18 +372,6 @@
             tokens, wp[0:512, :], NT, preferred_element_type=F32
         ).astype(BF16)
 
-    for copy in local[2:]:
-        copy.wait()
-    rest = w_1.shape[0] - 1024
-    mine = pl.ds(pl.multiple_of((y * 4 + x) * 144, 16), 144)
-    cross = remote(f_own.at[mine], f_far.at[mine], f_send.at[0], f_recv.at[0], mirror=True)
-    cross_v = remote(bias_own, bias_far, f_send.at[1], f_recv.at[1], mirror=True)
-    real = lax.broadcasted_iota(jnp.int32, (128, WIDTH), 0) < rest
-    f_own[1024:1152, :] = jnp.where(real, tail_1[...], jnp.zeros((128, WIDTH), BF16))
-    f_own[2176:2304, :] = jnp.where(real, tail_2[...], jnp.zeros((128, WIDTH), BF16))
-    cross.start()
-    cross_v.start()
-
     project(0, x)
     project(1, left)
     project(2, right)
@@ -344,6 +423,14 @@
     on_right.wait_recv()
     on_left.wait_recv()
     project(3, far_x)
+    each_core(pass_b)
+    each_core(take_b)
+    for k in range(3):
+        bx_copy(k).start()
+    cross.wait_recv()
+    for part in (0, 1):
+        start_first(part)
+        start_second(part, 0)
     for copy in copies_s:
         copy.wait_recv()
     seg_up = remote(segs.at[1], segs.at[0], s_send.at[3], s_recv.at[3], dz=1)
@@ -351,67 +438,6 @@
     pl.when(has_next)(seg_up.start)
     pl.when(has_prev)(seg_down.start)
 
-    B_CUTS = ((0, 48), (48, 32))
-
-    def rows_of(owner, core):
-        first, rows = B_CUTS[core]
-        return pl.ds(pl.multiple_of(owner * 80 + first, 16), rows)
-
-    def b_copies(core):
-        ref = wof.at[x, rows_of(zl, core)]
-        return [
-            remote(ref, ref, b_send.at[k], b_recv.at[k], dz=dz)
-            for k, dz in enumerate((1, -1, (2, -2)[core]))
-        ]
-
-    def bs_copies(core):
-        made = []
-        for k, d in enumerate((-1, 1, 2)):
-            ref = wof.at[x, rows_of(around(zl, d), core)]
-            made.append(remote(ref, ref, bs_send.at[k], bs_recv.at[k], dc=1))
-        return made
-
-    def each_core(act):
-        for core in (0, 1):
-
-            @pl.when(c == core)
-            def _():
-                act(core)
-
-    def start_b(core):
-        for copy in b_copies(core):
-            copy.start()
-
-    def pass_b(core):
-        for copy in b_copies(core):
-            copy.wait_recv()
-        for copy in bs_copies(core):
-            copy.start()
-
-    def take_b(core):
-        for copy in bs_copies(1 - core):
-            copy.wait_recv()
-
-    def end_b(core):
-        for copy in b_copies(core) + bs_copies(core):
-            copy.wait_send()
-
-    half_o = pl.ds(pl.multiple_of(c * 160, 16), 160)
-
-    def bx_copy(k):
-        ref = wof.at[x, half_o]
-        return remote(ref, ref, bx_send.at[k], bx_recv.at[k], dx=(1, -1, 2)[k])
-
-    def bxs_copy(k):
-        ref = wof.at[around(x, (-1, 1, 2)[k]), half_o]
-        return remote(ref, ref, bx_send.at[3 + k], bx_recv.at[3 + k], dc=1)
-
-    each_core(start_b)
-
-    cross.wait_recv()
-    for part in (0, 1):
-        start_first(part)
-        start_second(part, 0)
 
     scale = 1.0 / math.sqrt(HEAD)
     seg_keys[0] = jnp.concatenate([segs[1, b][:, :TOK] for b in range(4)] + [segs[1, 0][:, :TOK]], axis=1)
@@ -453,10 +479,6 @@
         for part in (1, 0):
             first_copy(part, k - 1).wait_recv()
             start_second(part, k)
-    each_core(pass_b)
-    each_core(take_b)
-    for k in range(3):
-        bx_copy(k).start()
     own_steps(2)
     for part in (1, 0):
         hand_on(part, 0)
@@ -536,7 +558,7 @@
             hid[:, at] = gelu(inner + biases[0:1, at]).astype(BF16)
             return carry
 
-        lax.fori_loop(0, 3, step, 0)
+        lax.fori_loop(0, 3, step, 0, unroll=True)
 
     def project_hidden(weights, first):
         def step(i, carry):
@@ -545,7 +567,7 @@
             mlp[:, at] = got if first else mlp[:, at] + got
             return carry
 
-        lax.fori_loop(0, 3, step, 0)
+        lax.fori_loop(0, 3, step, 0, unroll=True)
 
     hidden_of(f_own, bias_own)
     project_hidden(f_own, True)
@@ -566,7 +588,7 @@
     back.wait_recv()
     out[...] = (mine_sum + mlp_in[...].astype(F32)).astype(BF16)
 
-    for copy in copies_a + copies_as + copies_n + copies_s:
+    for copy in copies_a + copies_ay + copies_as + copies_n + copies_s:
         copy.wait_send()
     for up, down in copies_k:
         pl.when(has_next)(up.wait_send)
@@ -625,7 +647,7 @@
         pltpu.VMEM((TOK, WIDTH), BF16),
         dma((4,)),
     ]
-    for shape in ((4,), (3,), (4,), (3,), (4,), (5,), (2, 4), (2,), (2, 3), (2, 4, 4), (6,), (3,), (2,)):
+    for shape in ((4,), (3, 3), (3,), (4,), (3,), (4,), (5,), (2, 4), (2,), (2, 3), (2, 4, 4), (6,), (3,), (2,)):
         scratch += [dma(shape), dma(shape)]
     return pl.pallas_call(
         layer_kernel,
@@ -674,7 +696,7 @@
         ln2_bias,
         out_bias,
         fc2_bias,
-        jnp.pad(fc1_bias, (0, WIDTH - fc1_bias.shape[0])),
+        fc1_bias,
         w_qkv.T,
         w_out,
         w_1,

time: 111 us -> 101 us (0.910)
  Pallas kernels: 107 us -> 97.4 us
  local copies, waits for them, and re-layouts: 3.09 us -> 1.81 us
    pallas_call x1, Pallas kernels: 107 us -> 97.4 us  [layer_call(): pl.pallas_call(layer_kernel, out_shape=jax.ShapeDtypeStruct((TOK, WIDTH),...]
    pad x1 -> x0, local copies, waits for them, and re-layouts: 1.28 us -> none  [per_device(): jnp.pad(fc1_bias, (0, WIDTH - fc1_bias.shape[0]))]
where the time goes in v4:
time: 101 us; the launch traced here: 99.2 us
  Pallas kernels  97.4 us (96%)
  local copies, waits for them, and re-layouts  1.81 us (2%)
    pallas_call x1, Pallas kernels, layer_call(): pl.pallas_call(layer_kernel, out_shape=jax.ShapeDtypeStruct((TOK, WIDTH),...  97.4 us

profile of v4, /device:TPU:1, one launch (start us, length us, event | category | flops | bytes accessed | tf_op | source)
XLA Modules:
  0.0 99.2 jit_solution(16505370154989871558)
XLA Ops:
  0.0 97.4 %encoder_layer.1 = bf16[192,1152]{1,0:T(8,128)(2,1)} custom-call(bf16[192,1152]{1,0:T(8,128)(2,1)} %bitcast.8, s32[1,192]{1,0:T(1,128)} %seg_in.1, s32[1,192]{1,0:T(1,128)} %rows_in.1, s32[1,192]{1,0:T(1,128)} %cols_in.1, bf16[64,1152]{1,0:T(8,128)(2,1)} %rows_tab.1, bf16[64,1152]{1,0:T(8,128)(2,1)} %cols_tab.1, f32[1152]{0:T(1024)} %ln1_gain.1, ...), custom_call_target="tpu_custom_call" | custom-call | tf_op jit(solution)/shard_map/encoder_layer/pallas_call | solution.py:652
  97.4 1.8 %copy.19 = bf16[1,192,1152]{2,1,0:T(8,128)(2,1)} copy(bf16[1,192,1152]{2,1,0:T(8,128)(2,1)} %bitcast.6) | data formatting | bytes 884736

commit v5 on v4

--- a/solution.py
+++ b/solution.py
@@ -372,11 +372,7 @@
             tokens, wp[0:512, :], NT, preferred_element_type=F32
         ).astype(BF16)
 
-    project(0, x)
-    project(1, left)
-    project(2, right)
-
-    PARTS = ((0, 96, 48), (96, 48, 32))
+    PARTS = ((0, 112, 64), (112, 32, 16))
     def held(part, k, db=0):
         d = (0, -1, 1, 2)[k]
         if part == 0:
@@ -420,17 +416,19 @@
             second_copy(part, k, i).wait_recv()
             hand_copy(part, k, i).start()
 
+    project(0, x)
+    cross.wait_recv()
+    for part in (0, 1):
+        start_first(part)
+        start_second(part, 0)
+    project(1, left)
+    project(2, right)
+
     on_right.wait_recv()
     on_left.wait_recv()
     project(3, far_x)
     each_core(pass_b)
     each_core(take_b)
-    for k in range(3):
-        bx_copy(k).start()
-    cross.wait_recv()
-    for part in (0, 1):
-        start_first(part)
-        start_second(part, 0)
     for copy in copies_s:
         copy.wait_recv()
     seg_up = remote(segs.at[1], segs.at[0], s_send.at[3], s_recv.at[3], dz=1)
@@ -474,14 +472,18 @@
 
         lax.fori_loop(first, first + 2, step, 0)
 
-    own_steps(0)
     for k in (1, 2, 3):
         for part in (1, 0):
             first_copy(part, k - 1).wait_recv()
             start_second(part, k)
+    for k in range(3):
+        bx_copy(k).start()
+    own_steps(0)
+    for part in (1, 0):
+        hand_on(part, 0)
     own_steps(2)
     for part in (1, 0):
-        hand_on(part, 0)
+        hand_on(part, 1)
 
     pl.when(has_prev)(seg_up.wait_recv)
     pl.when(has_next)(seg_down.wait_recv)
@@ -525,8 +527,9 @@
             @pl.when(k == step)
             def _():
                 mixed_copy(step).start()
-                for part in (1, 0):
-                    hand_on(part, step + 1)
+                if step < 2:
+                    for part in (1, 0):
+                        hand_on(part, step + 2)
                 bx_copy(step).wait_recv()
                 bxs_copy(step).start()
 

time: 101 us -> 93.6 us (0.927)
  Pallas kernels: 97.4 us -> 90.5 us
    pallas_call x1, Pallas kernels: 97.4 us -> 90.5 us  [layer_call(): pl.pallas_call(layer_kernel, out_shape=jax.ShapeDtypeStruct((TOK, WIDTH),...]
where the time goes in v5:
time: 93.6 us; the launch traced here: 92.3 us
  Pallas kernels  90.5 us (97%)
  local copies, waits for them, and re-layouts  1.81 us (2%)
    pallas_call x1, Pallas kernels, layer_call(): pl.pallas_call(layer_kernel, out_shape=jax.ShapeDtypeStruct((TOK, WIDTH),...  90.5 us

profile of v5, /device:TPU:1, one launch (start us, length us, event | category | flops | bytes accessed | tf_op | source)
XLA Modules:
  0.0 92.3 jit_solution(4160021758513713762)
XLA Ops:
  0.0 90.5 %encoder_layer.1 = bf16[192,1152]{1,0:T(8,128)(2,1)} custom-call(bf16[192,1152]{1,0:T(8,128)(2,1)} %bitcast.8, s32[1,192]{1,0:T(1,128)} %seg_in.1, s32[1,192]{1,0:T(1,128)} %rows_in.1, s32[1,192]{1,0:T(1,128)} %cols_in.1, bf16[64,1152]{1,0:T(8,128)(2,1)} %rows_tab.1, bf16[64,1152]{1,0:T(8,128)(2,1)} %cols_tab.1, f32[1152]{0:T(1024)} %ln1_gain.1, ...), custom_call_target="tpu_custom_call" | custom-call | tf_op jit(solution)/shard_map/encoder_layer/pallas_call | solution.py:655
  90.5 1.8 %copy.19 = bf16[1,192,1152]{2,1,0:T(8,128)(2,1)} copy(bf16[1,192,1152]{2,1,0:T(8,128)(2,1)} %bitcast.6) | data formatting | bytes 884736

commit v6 on v5

--- a/solution.py
+++ b/solution.py
@@ -300,11 +300,16 @@
 
     def bx_copy(k):
         ref = wof.at[x, half_o]
-        return remote(ref, ref, bx_send.at[k], bx_recv.at[k], dx=(1, -1, 2)[k])
+        return remote(ref, ref, bx_send.at[k], bx_recv.at[k], dx=(1, -1)[k])
+
+    def bx_hand(k):
+        at = pl.ds(pl.multiple_of(c * 160 + 80 * k, 16), 80)
+        ref = wof.at[around(x, (-1, 1)[k]), at]
+        return remote(ref, ref, bx_send.at[2 + k], bx_recv.at[2 + k], dx=(1, -1)[k])
 
     def bxs_copy(k):
         ref = wof.at[around(x, (-1, 1, 2)[k]), half_o]
-        return remote(ref, ref, bx_send.at[3 + k], bx_recv.at[3 + k], dc=1)
+        return remote(ref, ref, bx_send.at[4 + k], bx_recv.at[4 + k], dc=1)
 
     each_core(start_b)
 
@@ -476,12 +481,16 @@
         for part in (1, 0):
             first_copy(part, k - 1).wait_recv()
             start_second(part, k)
-    for k in range(3):
+    for k in range(2):
         bx_copy(k).start()
     own_steps(0)
     for part in (1, 0):
         hand_on(part, 0)
     own_steps(2)
+    for k in range(2):
+        bx_copy(k).wait_recv()
+        bx_hand(k).start()
+        bxs_copy(k).start()
     for part in (1, 0):
         hand_on(part, 1)
 
@@ -530,8 +539,10 @@
                 if step < 2:
                     for part in (1, 0):
                         hand_on(part, step + 2)
-                bx_copy(step).wait_recv()
-                bxs_copy(step).start()
+                if step == 1:
+                    bx_hand(0).wait_recv()
+                    bx_hand(1).wait_recv()
+                    bxs_copy(2).start()
 
         return carry
 
@@ -601,8 +612,10 @@
     for copy in [cross, cross_v, give, back, on_right, on_left]:
         copy.wait_send()
     each_core(end_b)
+    for k in range(2):
+        bx_copy(k).wait_send()
+        bx_hand(k).wait_send()
     for k in range(3):
-        bx_copy(k).wait_send()
         bxs_copy(k).wait_send()
         mixed_copy(k).wait_send()
     for part in (0, 1):
@@ -650,7 +663,7 @@
         pltpu.VMEM((TOK, WIDTH), BF16),
         dma((4,)),
     ]
-    for shape in ((4,), (3, 3), (3,), (4,), (3,), (4,), (5,), (2, 4), (2,), (2, 3), (2, 4, 4), (6,), (3,), (2,)):
+    for shape in ((4,), (3, 3), (3,), (4,), (3,), (4,), (5,), (2, 4), (2,), (2, 3), (2, 4, 4), (7,), (3,), (2,)):
         scratch += [dma(shape), dma(shape)]
     return pl.pallas_call(
         layer_kernel,

time: 93.6 us -> 89.8 us (0.959)
  Pallas kernels: 90.5 us -> 87 us
    pallas_call x1, Pallas kernels: 90.5 us -> 87 us  [layer_call(): pl.pallas_call(layer_kernel, out_shape=jax.ShapeDtypeStruct((TOK, WIDTH),...]
where the time goes in v6:
time: 89.8 us; the launch traced here: 88.8 us
  Pallas kernels  87 us (97%)
  local copies, waits for them, and re-layouts  1.81 us (2%)
    pallas_call x1, Pallas kernels, layer_call(): pl.pallas_call(layer_kernel, out_shape=jax.ShapeDtypeStruct((TOK, WIDTH),...  87 us
    unnamed x1, local copies, waits for them, and re-layouts  1.81 us

profile of v6, /device:TPU:1, one launch (start us, length us, event | category | flops | bytes accessed | tf_op | source)
XLA Modules:
  0.0 88.8 jit_solution(3013370541938436615)
XLA Ops:
  0.0 87.0 %encoder_layer.1 = bf16[192,1152]{1,0:T(8,128)(2,1)} custom-call(bf16[192,1152]{1,0:T(8,128)(2,1)} %bitcast.8, s32[1,192]{1,0:T(1,128)} %seg_in.1, s32[1,192]{1,0:T(1,128)} %rows_in.1, s32[1,192]{1,0:T(1,128)} %cols_in.1, bf16[64,1152]{1,0:T(8,128)(2,1)} %rows_tab.1, bf16[64,1152]{1,0:T(8,128)(2,1)} %cols_tab.1, f32[1152]{0:T(1024)} %ln1_gain.1, ...), custom_call_target="tpu_custom_call" | custom-call | tf_op jit(solution)/shard_map/encoder_layer/pallas_call | solution.py:668
  87.0 1.8 %copy.19 = bf16[1,192,1152]{2,1,0:T(8,128)(2,1)} copy(bf16[1,192,1152]{2,1,0:T(8,128)(2,1)} %bitcast.6) | data formatting | bytes 884736

commit v7 on v6

--- a/solution.py
+++ b/solution.py
@@ -390,8 +390,15 @@
     def first_copy(part, i):
         first, rows, _ = PARTS[part]
         ref = unit(y, x, first, rows)
-        d = (1, -1, 2)[i]
+        d = (1, -1)[i]
         return remote(ref, ref, f1_send.at[part, i], f1_recv.at[part, i], **along(part, 0, d))
+
+    def first_hand(part, i):
+        first, rows, half = PARTS[part]
+        cut = ((first, half), (first + half, rows - half))[i]
+        ref = unit(*held(part, 1 + i), *cut)
+        at = (part, 2 + i)
+        return remote(ref, ref, f1_send.at[at], f1_recv.at[at], **along(part, 0, (1, -1)[i]))
 
     def second_copy(part, k, i):
         first, rows, _ = PARTS[part]
@@ -409,7 +416,7 @@
         return remote(ref, ref, f2_send.at[at], f2_recv.at[at], **along(part, 1, d))
 
     def start_first(part):
-        for i in range(3):
+        for i in range(2):
             first_copy(part, i).start()
 
     def start_second(part, k):
@@ -479,7 +486,12 @@
 
     for k in (1, 2, 3):
         for part in (1, 0):
-            first_copy(part, k - 1).wait_recv()
+            if k < 3:
+                first_copy(part, k - 1).wait_recv()
+                first_hand(part, k - 1).start()
+            else:
+                first_hand(part, 0).wait_recv()
+                first_hand(part, 1).wait_recv()
             start_second(part, k)
     for k in range(2):
         bx_copy(k).start()
@@ -619,8 +631,9 @@
         bxs_copy(k).wait_send()
         mixed_copy(k).wait_send()
     for part in (0, 1):
-        for i in range(3):
+        for i in range(2):
             first_copy(part, i).wait_send()
+            first_hand(part, i).wait_send()
         for k in range(4):
             for i in range(2):
                 second_copy(part, k, i).wait_send()
@@ -663,7 +676,7 @@
         pltpu.VMEM((TOK, WIDTH), BF16),
         dma((4,)),
     ]
-    for shape in ((4,), (3, 3), (3,), (4,), (3,), (4,), (5,), (2, 4), (2,), (2, 3), (2, 4, 4), (7,), (3,), (2,)):
+    for shape in ((4,), (3, 3), (3,), (4,), (3,), (4,), (5,), (2, 4), (2,), (2, 4), (2, 4, 4), (7,), (3,), (2,)):
         scratch += [dma(shape), dma(shape)]
     return pl.pallas_call(
         layer_kernel,

time: 89.8 us -> 92.6 us (1.031)
  Pallas kernels: 87 us -> 89.7 us
    pallas_call x1, Pallas kernels: 87 us -> 89.7 us  [layer_call(): pl.pallas_call(layer_kernel, out_shape=jax.ShapeDtypeStruct((TOK, WIDTH),...]
where the time goes in v7:
time: 92.6 us; the launch traced here: 91.5 us
  Pallas kernels  89.7 us (97%)
  local copies, waits for them, and re-layouts  1.81 us (2%)
    pallas_call x1, Pallas kernels, layer_call(): pl.pallas_call(layer_kernel, out_shape=jax.ShapeDtypeStruct((TOK, WIDTH),...  89.7 us

profile of v7, /device:TPU:1, one launch (start us, length us, event | category | flops | bytes accessed | tf_op | source)
XLA Modules:
  0.0 91.5 jit_solution(13552487284873497841)
XLA Ops:
  0.0 89.7 %encoder_layer.1 = bf16[192,1152]{1,0:T(8,128)(2,1)} custom-call(bf16[192,1152]{1,0:T(8,128)(2,1)} %bitcast.8, s32[1,192]{1,0:T(1,128)} %seg_in.1, s32[1,192]{1,0:T(1,128)} %rows_in.1, s32[1,192]{1,0:T(1,128)} %cols_in.1, bf16[64,1152]{1,0:T(8,128)(2,1)} %rows_tab.1, bf16[64,1152]{1,0:T(8,128)(2,1)} %cols_tab.1, f32[1152]{0:T(1024)} %ln1_gain.1, ...), custom_call_target="tpu_custom_call" | custom-call | tf_op jit(solution)/shard_map/encoder_layer/pallas_call | solution.py:681
  89.7 1.8 %copy.19 = bf16[1,192,1152]{2,1,0:T(8,128)(2,1)} copy(bf16[1,192,1152]{2,1,0:T(8,128)(2,1)} %bitcast.6) | data formatting | bytes 884736
